TPU v7x, 256 devices: a whole 4x4x8 slice. The times are simulated.
256 devices in a mesh: frame: 32 (over x_lo, z, core), mod: 8 (over y, x_hi).
Axes of the slice: x: 4 (x_hi: 2, x_lo: 2; x = x_hi * 2 + x_lo), y: 4, z: 8, core: 2. Of those that a mesh axis runs over, the one named last changes fastest.
Arguments:
- frames: bfloat16 [4096, 32768], P('frame', 'mod'), may hold values from 0.2 to 64, as said below
- cycle_label: int32 [32768], P('mod'), may hold values from 0 to 15, as said below
- good_pixel: int32 [32768], P('mod'), may hold values from 0 to 1
Outputs:
- correlation: float32 [16, 4096, 1024], P('mod', 'frame')
Inputs may be any that keep to these rules, and one draw needn't show every extreme that they name: `cycle_label`: on every block of 4096 consecutive pixels each of the 16 cycles holds exactly 256 pixels, at least one of them with good_pixel 1. `frames`: positive intensities.
All inputs are finite; a program needn't handle non-finite values.
Results may differ from a plain program's by a relative error of at most 0.0003.
Values may be sent and summed in bfloat16 or wider, within the bound.
A program may use at most 64 MiB of HBM per device.

v0:
```python
import jax
import jax.numpy as jnp
from jax import lax
from jax.sharding import PartitionSpec as P

CYCLES = 16
LAG = 1024


def passed_along(value, axis, steps):
    count = lax.axis_size(axis)
    first, last = (max(0, -steps), min(count, count - steps))
    return lax.ppermute(value, axis, [(source, source + steps) for source in range(first, last)])


def frame_window(frame_block):
    distance_count = LAG // frame_block.shape[0]
    pieces = [frame_block]
    for distance in range(1, distance_count + 1):
        pieces.append(passed_along(frame_block, "frame", -distance))
    return jnp.concatenate(pieces, axis=0)


def correlate(gram_tile, window_sums, cycle_counts):
    block_rows = gram_tile.shape[1]
    window_width = gram_tile.shape[2]
    frame_at = lax.axis_index("frame") * block_rows + jnp.arange(window_width, dtype=jnp.int32)
    in_range = frame_at < block_rows * lax.axis_size("frame")
    earlier = window_sums[:, :block_rows]
    safe_sums = jnp.where(in_range[None, :], window_sums, 1.0)
    normalized = (
        gram_tile * cycle_counts[:, None, None] / (earlier[:, :, None] * safe_sums[:, None, :])
    )
    normalized = jnp.where(in_range[None, None, :], normalized, 0.0)
    cycle_number = normalized.shape[0]
    flattened = jnp.pad(
        normalized.reshape(cycle_number, block_rows * window_width), ((0, 0), (0, block_rows))
    )
    return flattened.reshape(cycle_number, block_rows, window_width + 1)[:, :, :LAG]


def shards(frames, cycle_label, good_pixel):
    mod_count = lax.axis_size("mod")
    cycle_dev = CYCLES // mod_count
    first_cycle = lax.axis_index("mod") * cycle_dev
    block_rows = frames.shape[0]
    pix_count = frames.shape[1]
    per_cycle = pix_count // CYCLES
    ordering = jnp.argsort(cycle_label, stable=True)
    sorted_frames = jnp.take(frames, ordering, axis=1)
    sorted_good = jnp.take(good_pixel, ordering, axis=0).astype(jnp.bfloat16)
    window = frame_window(sorted_frames)
    window_width = window.shape[0]
    block_three = sorted_frames.reshape(block_rows, CYCLES, per_cycle)
    good_two = sorted_good.reshape(CYCLES, per_cycle)
    window_three = window.reshape(window_width, CYCLES, per_cycle)
    weighted = block_three * good_two[None]
    gram_tile = lax.psum_scatter(
        jnp.einsum("frc,grc->rfg", weighted, window_three, preferred_element_type=jnp.float32),
        "mod",
        scatter_dimension=0,
        tiled=True,
    )
    partial_sums = jnp.einsum(
        "grc,rc->gr", window_three, good_two, preferred_element_type=jnp.float32
    )
    partial_counts = jnp.sum(good_two.astype(jnp.float32), axis=1)
    all_sums, all_counts = lax.psum((partial_sums, partial_counts), "mod")
    window_sums = lax.dynamic_slice_in_dim(all_sums, first_cycle, cycle_dev, 1).T
    cycle_counts = lax.dynamic_slice_in_dim(all_counts, first_cycle, cycle_dev, 0)
    return correlate(gram_tile, window_sums, cycle_counts)


def solution(mesh):
    placed = (P("frame", "mod"), P("mod"), P("mod"))
    return jax.shard_map(
        shards, mesh=mesh, in_specs=placed, out_specs=P("mod", "frame", None), check_vma=False
    )
```

profile of v0, /device:TPU:1, one launch (start us, length us, event | category | flops | bytes accessed | tf_op | source)
XLA Modules:
  0.0 616.7 jit_solution(17780246840133231440)
XLA Ops:
  6.5 6.5 %sort.17 = (s32[4096]{0:T(1024)}, s32[4096]{0:T(1024)S(1)}) sort(s32[4096]{0:T(1024)} %param.4, s32[4096]{0:T(1024)S(1)} %iota.12), dimensions={0}, to_apply=%region_0.0 | sort | flops 49152 | bytes 65536 | tf_op jit(solution)/shard_map/jit(argsort)/sort | solution.py:49
  13.1 1.6 copy.6
  14.7 12.1 %gather_fusion = bf16[4096,128]{1,0:T(8,128)(2,1)S(1)} fusion(bf16[128,4096]{0,1:T(8,128)(2,1)S(1)} %copy.6, s32[4096]{0:T(1024)S(1)} %fusion.8), kind=kCustom, calls=%fused_computation | custom fusion | bytes 2113536 | tf_op jit(solution)/shard_map/jit(_take)/gather | solution.py:50
  26.8 3.0 constant_dynamic-update-slice_fusion.8
  29.8 5.1 collective-permute-start
  34.9 1.3 collective-permute-start.1
  36.2 1.3 collective-permute-start.2
  40.1 23.0 %gather_fusion.1 = s32[4096]{0:T(1024)S(1)} fusion(s32[4096]{0:T(1024)S(1)} %copy-done, s32[4096]{0:T(1024)S(1)} %fusion.8), kind=kCustom, calls=%fused_computation.1 | custom fusion | bytes 49152 | tf_op jit(solution)/shard_map/jit(_take)/gather | solution.py:51
  65.2 2.3 constant_dynamic-update-slice_fusion.7
  68.8 2.4 constant_dynamic-update-slice_fusion.6
  71.2 78.3 %collective-permute-done.2 = bf16[128,4096]{0,1:T(8,128)(2,1)} collective-permute-done((bf16[128,4096]{0,1:T(8,128)(2,1)S(1)}, bf16[128,4096]{0,1:T(8,128)(2,1)}, u32[]{:S(2)}, u32[]{:S(2)}) %collective-permute-start.2) | collective-permute-done | bytes 1048608 | tf_op jit(solution)/shard_map/ppermute | solution.py:13
  150.8 2.4 constant_dynamic-update-slice_fusion.5
  153.2 2.4 constant_dynamic-update-slice_fusion.4
  155.6 42.3 %collective-permute-done.4 = bf16[128,4096]{0,1:T(8,128)(2,1)} collective-permute-done((bf16[128,4096]{0,1:T(8,128)(2,1)S(1)}, bf16[128,4096]{0,1:T(8,128)(2,1)}, u32[]{:S(2)}, u32[]{:S(2)}) %collective-permute-start.4) | collective-permute-done | bytes 1048608 | tf_op jit(solution)/shard_map/ppermute | solution.py:13
  197.9 2.4 constant_dynamic-update-slice_fusion.3
  200.2 1.4 collective-permute-done.5
  203.9 43.6 %collective-permute-done.7 = bf16[128,4096]{0,1:T(8,128)(2,1)S(1)} collective-permute-done((bf16[128,4096]{0,1:T(8,128)(2,1)S(1)}, bf16[128,4096]{0,1:T(8,128)(2,1)S(1)}, u32[]{:S(2)}, u32[]{:S(2)}) %collective-permute-start.7) | collective-permute-done | bytes 1048608 | tf_op jit(solution)/shard_map/ppermute | solution.py:13
  248.6 5.0 fusion.6
  254.3 8.9 %fusion = f32[16,128,1152]{2,1,0:T(8,128)} fusion(bf16[1152,16,256]{0,2,1:T(8,128)(2,1)} %bitcast.21, bf16[128,16,256]{2,0,1:T(8,128)(2,1)S(1)} %copy.7, pred[16,256]{1,0:T(8,128)(4,1)S(1)} %broadcast_in_dim.54, bf16[16,256]{1,0:T(8,128)(2,1)S(1)} %get-tuple-element.8), kind=kOutput, calls=%fused_computation.4 | convolution fusion | flops 1209008128 | bytes 19935232 | tf_op jit(solution)/shard_map/frc,grc->rfg/dot_general | solution.py:59
  263.2 20.8 %psum.14 = f32[16]{0:T(128)S(1)} all-reduce(f32[16]{0:T(128)S(1)} %get-tuple-element.7), channel_id=1, replica_groups=mesh['frame'=32,'mod'=8] {'mod'}, use_global_device_ids=true, to_apply=%region_3.4 | all-reduce | flops 16 | bytes 128 | tf_op jit(solution)/shard_map/psum | solution.py:68
  284.1 186.1 %all-reduce.3.cloned.1.call-done = f32[1152,16]{0,1:T(8,128)} async-done(((f32[1152,16]{0,1:T(8,128)}), f32[1152,16]{0,1:T(8,128)}) %all-reduce.3.cloned.1.call-update) | async-done | bytes 73744 | tf_op jit(solution)/shard_map/psum | solution.py:68
  471.0 133.2 %reduce-scatter.2.cloned.1.call-done = f32[2,128,1152]{2,1,0:T(8,128)} async-done(((f32[16,128,1152]{2,1,0:T(8,128)}), f32[2,128,1152]{2,1,0:T(8,128)}) %reduce-scatter.2.cloned.1.call-update) | async-done | bytes 1179664 | tf_op jit(solution)/shard_map/reduce_scatter | solution.py:58
  604.2 1.7 select_bitcast_fusion
  607.3 1.5 reshape.52
  (33 shorter events, 14.7 us)
Async XLA Ops:
  6.5 33.6 %copy-start = (s32[4096]{0:T(1024)S(1)}, s32[4096]{0:T(1024)}, u32[]{:S(2)}) copy-start(s32[4096]{0:T(1024)} %param.5) | copy-start | bytes 49156
  6.5 463.6 %all-reduce.3.cloned.1.call-start = ((), (), s32[]{:S(2)}) async-start(), calls=%async_computation.2 | async-start | bytes 147456 | tf_op jit(solution)/shard_map/psum | solution.py:68
  29.8 34.0 %collective-permute-start = (bf16[128,4096]{0,1:T(8,128)(2,1)S(1)}, bf16[128,4096]{0,1:T(8,128)(2,1)}, u32[]{:S(2)}, u32[]{:S(2)}) collective-permute-start(bf16[128,4096]{0,1:T(8,128)(2,1)S(1)} %get-tuple-element.12), channel_id=1, source_target_pairs={{8,0},{16,8},{24,16},{32,24},{40,32},{48,40},{56,48},{64,56},{72,6... | collective-permute-start | bytes 3145736 | tf_op jit(solution)/shard_map/ppermute | solution.py:13
  34.9 32.6 %collective-permute-start.1 = (bf16[128,4096]{0,1:T(8,128)(2,1)S(1)}, bf16[128,4096]{0,1:T(8,128)(2,1)}, u32[]{:S(2)}, u32[]{:S(2)}) collective-permute-start(bf16[128,4096]{0,1:T(8,128)(2,1)S(1)} %get-tuple-element.12), channel_id=1, source_target_pairs={{16,0},{24,8},{32,16},{40,24},{48,32},{56,40},{64,48},{72,56},{80,... | collective-permute-start | bytes 3145736 | tf_op jit(solution)/shard_map/ppermute | solution.py:13
  36.2 113.3 %collective-permute-start.2 = (bf16[128,4096]{0,1:T(8,128)(2,1)S(1)}, bf16[128,4096]{0,1:T(8,128)(2,1)}, u32[]{:S(2)}, u32[]{:S(2)}) collective-permute-start(bf16[128,4096]{0,1:T(8,128)(2,1)S(1)} %get-tuple-element.12), channel_id=1, source_target_pairs={{24,0},{32,8},{40,16},{48,24},{56,32},{64,40},{72,48},{80,56},{88,... | collective-permute-start | bytes 3145736 | tf_op jit(solution)/shard_map/ppermute | solution.py:13
  37.5 115.7 %collective-permute-start.3 = (bf16[128,4096]{0,1:T(8,128)(2,1)S(1)}, bf16[128,4096]{0,1:T(8,128)(2,1)}, u32[]{:S(2)}, u32[]{:S(2)}) collective-permute-start(bf16[128,4096]{0,1:T(8,128)(2,1)S(1)} %get-tuple-element.12), channel_id=1, source_target_pairs={{32,0},{40,8},{48,16},{56,24},{64,32},{72,40},{80,48},{88,56},{96,... | collective-permute-start | bytes 3145736 | tf_op jit(solution)/shard_map/ppermute | solution.py:13
  38.8 159.1 %collective-permute-start.4 = (bf16[128,4096]{0,1:T(8,128)(2,1)S(1)}, bf16[128,4096]{0,1:T(8,128)(2,1)}, u32[]{:S(2)}, u32[]{:S(2)}) collective-permute-start(bf16[128,4096]{0,1:T(8,128)(2,1)S(1)} %get-tuple-element.12), channel_id=1, source_target_pairs={{40,0},{48,8},{56,16},{64,24},{72,32},{80,40},{88,48},{96,56},{104... | collective-permute-start | bytes 3145736 | tf_op jit(solution)/shard_map/ppermute | solution.py:13
  63.9 137.8 %collective-permute-start.5 = (bf16[128,4096]{0,1:T(8,128)(2,1)S(1)}, bf16[128,4096]{0,1:T(8,128)(2,1)S(1)}, u32[]{:S(2)}, u32[]{:S(2)}) collective-permute-start(bf16[128,4096]{0,1:T(8,128)(2,1)S(1)} %get-tuple-element.12), channel_id=1, source_target_pairs={{48,0},{56,8},{64,16},{72,24},{80,32},{88,40},{96,48},{104,56},{11... | collective-permute-start | bytes 3145736 | tf_op jit(solution)/shard_map/ppermute | solution.py:13
  67.5 135.2 %collective-permute-start.6 = (bf16[128,4096]{0,1:T(8,128)(2,1)S(1)}, bf16[128,4096]{0,1:T(8,128)(2,1)S(1)}, u32[]{:S(2)}, u32[]{:S(2)}) collective-permute-start(bf16[128,4096]{0,1:T(8,128)(2,1)S(1)} %get-tuple-element.12), channel_id=1, source_target_pairs={{56,0},{64,8},{72,16},{80,24},{88,32},{96,40},{104,48},{112,56},{1... | collective-permute-start | bytes 3145736 | tf_op jit(solution)/shard_map/ppermute | solution.py:13
  149.5 98.0 %collective-permute-start.7 = (bf16[128,4096]{0,1:T(8,128)(2,1)S(1)}, bf16[128,4096]{0,1:T(8,128)(2,1)S(1)}, u32[]{:S(2)}, u32[]{:S(2)}) collective-permute-start(bf16[128,4096]{0,1:T(8,128)(2,1)S(1)} %get-tuple-element.12), channel_id=1, source_target_pairs={{64,0},{72,8},{80,16},{88,24},{96,32},{104,40},{112,48},{120,56},{... | collective-permute-start | bytes 3145736 | tf_op jit(solution)/shard_map/ppermute | solution.py:13
  254.2 349.9 %reduce-scatter.2.cloned.1.call-start = ((), (), s32[]{:S(2)}) async-start(), calls=%async_computation.1 | async-start | bytes 10616832 | tf_op jit(solution)/shard_map/reduce_scatter | solution.py:58
Sparse Core Ops, SparseCore 0:
  254.4 215.7 all-reduce.2
  474.3 129.8 reduce-scatter.1
where the time goes:
time: 617 us
  waiting for transfers between devices  485 us (79%)
  local copies, waits for them, and re-layouts  57.2 us (9%)
  blocking collectives  20.8 us (3%)
  starting transfers between devices  14.2 us (2%)
  matrix products  13.9 us (2%)
  between operations  13.6 us (2%)
  other arithmetic  12.1 us (2%)
    psum x1, waiting for transfers between devices, shards(): all_sums, all_counts = lax.psum((partial_sums, partial_counts), 'mod')  186 us
    ppermute x8, waiting for transfers between devices, passed_along(): lax.ppermute(value, axis, [(source, source + steps) for source in range(f...  166 us
    reduce_scatter x1, waiting for transfers between devices, shards(): lax.psum_scatter(jnp.einsum('frc,grc->rfg', weighted, window_three, prefe...  133 us
    gather x2, local copies, waits for them, and re-layouts, shards(): sorted_good = jnp.take(good_pixel, ordering, axis=0).astype(jnp.bfloat16)  23 us
    psum x1, blocking collectives, shards(): all_sums, all_counts = lax.psum((partial_sums, partial_counts), 'mod')  20.8 us
    unnamed x11, local copies, waits for them, and re-layouts  16.6 us
    ppermute x8, starting transfers between devices, passed_along(): lax.ppermute(value, axis, [(source, source + steps) for source in range(f...  14.1 us
    gather x2, local copies, waits for them, and re-layouts, shards(): sorted_frames = jnp.take(frames, ordering, axis=1)  12.7 us
  transfers between devices with their start and end apart: 10, of which 7 were waited for; matrix products, arithmetic and copies ran while one was open for 8% of the time, Pallas kernels for 0%

commit v1 on v0

v1 whole, which is shorter than its diff:
```python
import functools

import jax
import jax.numpy as jnp
from jax import lax
from jax.experimental import pallas as pl
from jax.experimental.pallas import tpu as pltpu
from jax.sharding import PartitionSpec as P

CYCLES = 16
LAG = 1024
MESH = pl.DeviceIdType.MESH
NT = (((1,), (1,)), ((), ()))


def nt_dot(a, b):
    return lax.dot_general(a, b, NT, preferred_element_type=jnp.float32)


def arrange_kernel(cycles, per_cycle, frames_ref, label_ref, good_ref, x_ref, count_ref, rank_ref):
    q = pl.program_id(0)
    rows, lanes = label_ref.shape

    @pl.when(q == 0)
    def _():
        label = label_ref[...]
        member = jnp.concatenate(
            [jnp.where(label == c, 1.0, 0.0) for c in range(cycles)], axis=0
        ).astype(jnp.bfloat16)
        before = lax.broadcasted_iota(jnp.int32, (lanes, lanes), 0)
        at = lax.broadcasted_iota(jnp.int32, (lanes, lanes), 1)
        upper = jnp.where(before < at, 1.0, 0.0).astype(jnp.bfloat16)
        in_row = jnp.dot(member, upper, preferred_element_type=jnp.float32)
        totals = jnp.dot(
            member, jnp.ones((lanes, lanes), jnp.bfloat16), preferred_element_type=jnp.float32
        ).astype(jnp.bfloat16)
        size = cycles * rows
        here = lax.broadcasted_iota(jnp.int32, (size, size), 0)
        there = lax.broadcasted_iota(jnp.int32, (size, size), 1)
        earlier = (here // rows == there // rows) & (there < here)
        above = jnp.dot(
            jnp.where(earlier, 1.0, 0.0).astype(jnp.bfloat16),
            totals,
            preferred_element_type=jnp.float32,
        )
        ranks = (in_row + above) * member.astype(jnp.float32)
        total = ranks[:rows]
        for c in range(1, cycles):
            total = total + ranks[c * rows : (c + 1) * rows]
        rank_ref[...] = jnp.where(good_ref[...] > 0, total, -1.0)

    rank = jnp.where(label_ref[...] == q, rank_ref[...], -1.0)
    place = lax.broadcasted_iota(jnp.int32, (per_cycle, lanes), 0).astype(jnp.float32)
    acc = None
    step = 2
    for r in range(0, rows, step):
        hot = jnp.concatenate(
            [
                jnp.where(place == rank[r + i : r + i + 1, :], 1.0, 0.0).astype(jnp.bfloat16)
                for i in range(step)
            ],
            axis=1,
        )
        term = nt_dot(frames_ref[:, r * lanes : (r + step) * lanes], hot)
        acc = term if acc is None else acc + term
    x_ref[0, 0] = acc.astype(jnp.bfloat16)
    count = jnp.sum(jnp.where(rank >= 0.0, 1.0, 0.0))
    mine = lax.broadcasted_iota(jnp.int32, count_ref.shape[1:], 0) == q % 2
    count_ref[0] = jnp.where(mine, count, count_ref[0])


def arrange(frames, label, good, per_cycle):
    rows, pixels = frames.shape
    lanes = 128
    packed = (pixels // lanes, lanes)
    cycles = pixels // per_cycle
    return pl.pallas_call(
        functools.partial(arrange_kernel, cycles, per_cycle),
        grid=(cycles,),
        in_specs=[
            pl.BlockSpec((rows, pixels), lambda q: (0, 0)),
            pl.BlockSpec(packed, lambda q: (0, 0)),
            pl.BlockSpec(packed, lambda q: (0, 0)),
        ],
        out_specs=[
            pl.BlockSpec((1, 1, rows, per_cycle), lambda q: (q % 2, q // 2, 0, 0)),
            pl.BlockSpec((1, 8, lanes), lambda q: (q // 2, 0, 0)),
        ],
        out_shape=[
            jax.ShapeDtypeStruct((2, cycles // 2, rows, per_cycle), jnp.bfloat16),
            jax.ShapeDtypeStruct((cycles // 2, 8, lanes), jnp.float32),
        ],
        scratch_shapes=[pltpu.VMEM(packed, jnp.float32)],
    )(frames, label.reshape(packed), good.reshape(packed))


def exchange_kernel(
    frame_count, mod_count, x_ref, c_ref, out_ref,
    held, counts, tiles, far, recv_sem, send_sem, count_send, count_recv, far_send, far_recv,
):
    f = lax.axis_index("frame")
    m = lax.axis_index("mod")
    core = f % 2
    chip = f // 2
    chips = frame_count // 2
    y_count = mod_count // 2
    y, x = m // 2, m % 2
    partner = f + 1 - 2 * core
    steps = 2 * mod_count

    has_up1, has_up2 = chip + 1 < chips, chip + 2 < chips
    has_dn1, has_dn2 = chip >= 1, chip >= 2

    own, down1, down2, up1, up2 = 4 + core, 6 + core, 8 + core, 2 + core, core
    other_down1, other_down2, other_own = 7 - core, 9 - core, 5 - core

    def peer(o, sign):
        dy, dx = o // 2, o % 2
        return ((y + sign * dy + y_count) % y_count) * 2 + (x + dx) % 2

    barrier = pltpu.get_barrier_semaphore()

    def greet(cond, fr, mo):
        @pl.when(cond)
        def _():
            pl.semaphore_signal(barrier, inc=1, device_id=(fr, mo), device_id_type=MESH)

    for o in range(1, mod_count):
        pl.semaphore_signal(barrier, inc=1, device_id=(f, peer(o, 1)), device_id_type=MESH)
    pl.semaphore_signal(barrier, inc=1, device_id=(partner, m), device_id_type=MESH)
    greet(has_up1, f + 2, m)
    greet(has_up2, f + 4, m)
    greet(has_dn1, f - 2, m)
    greet(has_dn2, f - 4, m)
    arrivals = mod_count
    for cond in (has_up1, has_up2, has_dn1, has_dn2):
        arrivals = arrivals + jnp.where(cond, 1, 0)
    pl.semaphore_wait(barrier, arrivals)

    def remote(src, dst, send, recv, fr, mo):
        return pltpu.make_async_remote_copy(
            src_ref=src, dst_ref=dst, send_sem=send, recv_sem=recv,
            device_id=(fr, mo), device_id_type=MESH,
        )

    def forward(from_slot, to_slot, k, lane, fr):
        remote(
            held.at[from_slot, k], held.at[to_slot, k], send_sem.at[lane],
            recv_sem.at[to_slot, k], fr, m,
        ).start()

    def arrived(slot, k):
        pltpu.make_async_copy(held.at[slot, k], held.at[slot, k], recv_sem.at[slot, k]).wait()

    for cyc in range(2):
        pltpu.make_async_copy(
            x_ref.at[cyc, m], held.at[own, cyc * mod_count], recv_sem.at[own, cyc * mod_count]
        ).start()
    pltpu.make_async_copy(c_ref.at[m], counts.at[0], count_recv.at[0]).start()

    def spread(cyc):
        @pl.loop(1, mod_count)
        def _(o):
            to = peer(o, -1)
            k = cyc * mod_count + o
            remote(
                x_ref.at[cyc, to], held.at[own, k], send_sem.at[0], recv_sem.at[own, k], f, to
            ).start()

    spread(0)
    spread(1)
    for o in range(1, mod_count):
        to = peer(o, -1)
        remote(c_ref.at[to], counts.at[o], count_send.at[o], count_recv.at[o], f, to).start()

    def step(k):
        @pl.when(k < steps)
        def _():
            arrived(own, k)

            @pl.when(has_dn1)
            def _():
                forward(own, down1, k, 1, f - 2)

            @pl.when(has_up1)
            def _():
                forward(own, up1, k, 2, f + 2)

            forward(own, own, k, 3, partner)

        k1 = k - 1

        @pl.when((k1 >= 0) & (k1 < steps))
        def _():
            @pl.when(has_up1)
            def _():
                arrived(down1, k1)

                @pl.when(has_dn1)
                def _():
                    forward(down1, down2, k1, 4, f - 2)

                forward(down1, down1, k1, 5, partner)

            @pl.when(has_dn1)
            def _():
                arrived(up1, k1)

                @pl.when(has_up1)
                def _():
                    forward(up1, up2, k1, 6, f + 2)

        k2 = k - 2

        @pl.when((k2 >= 0) & (k2 < steps) & has_up2)
        def _():
            arrived(down2, k2)
            forward(down2, down2, k2, 7, partner)

    def product(lhs_slot, rhs_slot, cyc):
        total, later, earlier = None, None, None
        ones = jnp.ones((128, 256), jnp.bfloat16)
        for o in range(mod_count):
            k = cyc * mod_count + o
            lhs = held[lhs_slot, k]
            rhs = held[rhs_slot : rhs_slot + 2, k].reshape(256, 256)
            a, b, c = nt_dot(lhs, rhs), nt_dot(ones[:8], rhs), nt_dot(lhs, ones)
            if total is None:
                total, later, earlier = a, b, c
            else:
                total, later, earlier = total + a, later + b, earlier + c
        count = counts[0]
        for o in range(1, mod_count):
            count = count + counts[o]
        count = count[cyc : cyc + 1]
        return [
            total[:, i * 128 : i * 128 + 128] * count
            / (earlier * later[0:1, i * 128 : i * 128 + 128])
            for i in range(2)
        ]

    def far_copy(kind, cyc):
        distance = 2 if kind == 0 else 4
        return remote(
            far.at[kind, cyc], tiles.at[cyc, pl.ds(6 + 2 * kind, 2)],
            far_send.at[kind, cyc], far_recv.at[kind, cyc], f - distance, m,
        )

    def compute(cyc):
        @pl.loop(0, mod_count)
        def _(o):
            k = cyc * mod_count + o
            arrived(other_own, k)

            @pl.when(has_up1)
            def _():
                arrived(other_down1, k)

            @pl.when(has_up2)
            def _():
                arrived(other_down2, k)

            @pl.when(has_dn2)
            def _():
                arrived(up2, k)

        for kind, slot, cond in ((1, up2, has_dn2 & has_up2), (0, up1, has_dn1 & has_up2)):
            @pl.when(cond)
            def _():
                for i, tile in enumerate(product(slot, 8, cyc)):
                    far[kind, cyc, i] = tile
                far_copy(kind, cyc).start()

        for piece, cond in ((0, None), (1, has_up1), (2, has_up2)):
            def fill(piece=piece):
                for i, tile in enumerate(product(own, 4 + 2 * piece, cyc)):
                    tiles[cyc, 2 * piece + i] = tile

            if cond is None:
                fill()
            else:
                pl.when(cond)(fill)

                @pl.when(jnp.logical_not(cond))
                def _():
                    tiles[cyc, 2 * piece : 2 * piece + 2] = jnp.zeros((2, 128, 128), jnp.float32)

    def finish(cyc):
        for kind, distance in ((0, 3), (1, 4)):
            @pl.when(chip + distance < chips)
            def _():
                far_copy(kind, cyc).wait_recv()

            @pl.when(chip + distance >= chips)
            def _():
                tiles[cyc, 6 + 2 * kind : 8 + 2 * kind] = jnp.zeros((2, 128, 128), jnp.float32)

        row = lax.broadcasted_iota(jnp.int32, (128, 128), 0)
        lane = lax.broadcasted_iota(jnp.int32, (128, 128), 1)
        inside = lane + row < 128

        def turned(j):
            tile = tiles[cyc, core + j]
            for bit in (1, 2, 4):
                tile = jnp.where(row // bit % 2 == 1, pltpu.roll(tile, 128 - bit, 1), tile)
            return jnp.concatenate(
                [tile[:8]] + [pltpu.roll(tile[r : r + 8], 128 - r, 1) for r in range(8, 128, 8)], axis=0
            )

        now = turned(0)
        for j in range(LAG // 128):
            later = turned(j + 1)
            out_ref[cyc, :, j * 128 : j * 128 + 128] = jnp.where(inside, now, later)
            now = later

    middle = mod_count + 4

    @pl.loop(0, middle)
    def _(k):
        step(k)

    for o in range(mod_count):
        pltpu.make_async_copy(counts.at[o], counts.at[o], count_recv.at[o]).wait()
    compute(0)

    @pl.loop(middle, steps + 2)
    def _(k):
        step(k)

    finish(0)
    compute(1)
    finish(1)

    def sent(lane, slot):
        pltpu.make_async_copy(held.at[slot], held.at[slot], send_sem.at[lane]).wait()

    for cyc in range(2):
        pltpu.make_async_copy(
            held.at[own, pl.ds(cyc * mod_count + 1, mod_count - 1)],
            held.at[own, pl.ds(cyc * mod_count + 1, mod_count - 1)],
            send_sem.at[0],
        ).wait()
    for o in range(1, mod_count):
        pltpu.make_async_copy(counts.at[o], counts.at[o], count_send.at[o]).wait()
    for lane, slot, cond in (
        (1, own, has_dn1), (2, own, has_up1), (3, own, None), (4, down1, has_up1 & has_dn1),
        (5, down1, has_up1), (6, up1, has_up1 & has_dn1), (7, down2, has_up2),
    ):
        if cond is None:
            sent(lane, slot)
        else:
            pl.when(cond)(functools.partial(sent, lane, slot))
    for cyc in range(2):
        for kind, cond in ((1, has_dn2 & has_up2), (0, has_dn1 & has_up2)):
            @pl.when(cond)
            def _():
                far_copy(kind, cyc).wait_send()


def exchange(x, c, frame_count, mod_count):
    rows, per_cycle = x.shape[2:]
    steps = 2 * mod_count
    return pl.pallas_call(
        functools.partial(exchange_kernel, frame_count, mod_count),
        out_shape=jax.ShapeDtypeStruct((2, rows, LAG), jnp.float32),
        in_specs=[pl.BlockSpec(memory_space=pltpu.VMEM)] * 2,
        out_specs=pl.BlockSpec(memory_space=pltpu.VMEM),
        scratch_shapes=[
            pltpu.VMEM((10, steps, rows, per_cycle), jnp.bfloat16),
            pltpu.VMEM((mod_count, 8, 128), jnp.float32),
            pltpu.VMEM((2, 10, 128, 128), jnp.float32),
            pltpu.VMEM((2, 2, 2, 128, 128), jnp.float32),
            pltpu.SemaphoreType.DMA((10, steps)),
            pltpu.SemaphoreType.DMA((8,)),
            pltpu.SemaphoreType.DMA((mod_count,)),
            pltpu.SemaphoreType.DMA((mod_count,)),
            pltpu.SemaphoreType.DMA((2, 2)),
            pltpu.SemaphoreType.DMA((2, 2)),
        ],
        compiler_params=pltpu.CompilerParams(
            collective_id=0, has_side_effects=True, vmem_limit_bytes=32 * 1024 * 1024
        ),
    )(x, c)


def shards(frames, cycle_label, good_pixel):
    mod_count = lax.axis_size("mod")
    per_cycle = frames.shape[1] // (2 * mod_count)
    x, c = arrange(frames, cycle_label, good_pixel, per_cycle)
    return exchange(x, c, lax.axis_size("frame"), mod_count)


def solution(mesh):
    placed = (P("frame", "mod"), P("mod"), P("mod"))
    return jax.shard_map(
        shards, mesh=mesh, in_specs=placed, out_specs=P("mod", "frame", None), check_vma=False
    )
```

time: 617 us -> 129 us (0.21)
  the two profiles are of different devices: /device:TPU:1 before, /device:TPU:6 now
where the time goes in v1:
time: 129 us
  Pallas kernels  126 us (98%)
  local copies, waits for them, and re-layouts  2.95 us (2%)
    pallas_call x1, Pallas kernels, exchange(): pl.pallas_call(functools.partial(exchange_kernel, frame_count, mod_count)...  110 us
    pallas_call x1, Pallas kernels, arrange(): pl.pallas_call(functools.partial(arrange_kernel, cycles, per_cycle), grid...  16.1 us
    unnamed x5, local copies, waits for them, and re-layouts  2.95 us

profile of v1, /device:TPU:6, one launch (start us, length us, event | category | flops | bytes accessed | tf_op | source)
XLA Modules:
  0.0 129.0 jit_solution(16195916860985405967)
XLA Ops:
  0.0 16.1 %shard_map.37 = (bf16[2,8,128,256]{3,2,1,0:T(8,128)(2,1)}, f32[8,8,128]{2,1,0:T(8,128)}) custom-call(bf16[128,4096]{1,0:T(8,128)(2,1)} %frames_ref.1, s32[32,128]{1,0:T(8,128)} %bitcast.2, s32[32,128]{1,0:T(8,128)} %bitcast.3), custom_call_target="tpu_custom_call" | custom-call | tf_op jit(solution)/shard_map/pallas_call | solution.py:77
  16.1 0.0 copy-start
  16.1 1.2 copy-done
  17.3 0.0 copy-start.1
  17.3 0.8 copy-done.1
  18.1 109.9 %shard_map.38 = f32[2,128,1024]{2,1,0:T(8,128)S(1)} custom-call(bf16[2,8,128,256]{3,2,1,0:T(8,128)(2,1)S(1)} %copy-done, f32[8,8,128]{2,1,0:T(8,128)S(1)} %copy-done.1), custom_call_target="tpu_custom_call" | custom-call | tf_op jit(solution)/shard_map/pallas_call | solution.py:363
  128.0 1.0 copy.5
Async XLA Ops:
  16.1 1.2 copy-start
  17.3 0.8 copy-start.1

commit v2 on v0

v2 whole, which is shorter than its diff:
```python
import functools

import jax
import jax.numpy as jnp
from jax import lax
from jax.experimental import pallas as pl
from jax.experimental.pallas import tpu as pltpu
from jax.sharding import PartitionSpec as P

CYCLES = 16
LAG = 1024
MESH = pl.DeviceIdType.MESH
NT = (((1,), (1,)), ((), ()))
RELAY_LAG = 3
SHARE_LAG = 6
FIRST_GRAM = 7


def nt_dot(a, b):
    return lax.dot_general(a, b, NT, preferred_element_type=jnp.float32)


def rank_pixels(label_ref, good_ref, place, partial, cycles, per_cycle):
    rows, lanes = label_ref.shape
    label = label_ref[...]
    good = good_ref[...] > 0
    member = jnp.concatenate([jnp.where(label == c, 1.0, 0.0) for c in range(cycles)], axis=0)
    before = lax.broadcasted_iota(jnp.int32, (lanes, lanes), 0)
    at = lax.broadcasted_iota(jnp.int32, (lanes, lanes), 1)
    upper = jnp.where(before < at, 1.0, 0.0).astype(jnp.bfloat16)
    ones = jnp.ones((lanes, lanes), jnp.bfloat16)
    packed = member.astype(jnp.bfloat16)
    in_row = jnp.dot(packed, upper, preferred_element_type=jnp.float32)
    totals = jnp.dot(packed, ones, preferred_element_type=jnp.float32).astype(jnp.bfloat16)
    size = cycles * rows
    here = lax.broadcasted_iota(jnp.int32, (size, size), 0)
    there = lax.broadcasted_iota(jnp.int32, (size, size), 1)
    earlier = jnp.where((here // rows == there // rows) & (there < here), 1.0, 0.0)
    above = jnp.dot(earlier.astype(jnp.bfloat16), totals, preferred_element_type=jnp.float32)
    ranks = (in_row + above) * member
    usable = jnp.where(good, 1.0, 0.0)
    partial[...] = jnp.zeros_like(partial)
    total = None
    for c in range(cycles):
        mine = slice(c * rows, (c + 1) * rows)
        total = ranks[mine] if total is None else total + ranks[mine]
        per_row = jnp.sum(member[mine] * usable, axis=0, keepdims=True)
        partial[c // 2, c % 2 : c % 2 + 1, :] = jnp.broadcast_to(
            jnp.sum(per_row, axis=1, keepdims=True), (1, lanes)
        )
    where = jnp.where(good, total + label.astype(jnp.float32) * per_cycle, -1.0)
    for r in range(rows):
        place[r * lanes : (r + 1) * lanes, :] = jnp.broadcast_to(where[r : r + 1], (lanes, lanes)).T


def kernel(
    frame_count, mod_count, frames_hbm, label_hbm, good_hbm, out_hbm,
    frames, label, good, place, partial, packed, held, counts, tiles, far, out,
    in_sem, out_sem, recv_sem, send_sem, count_send, count_recv, far_send, far_recv,
):
    f = lax.axis_index("frame")
    m = lax.axis_index("mod")
    core = f % 2
    chip = f // 2
    chips = frame_count // 2
    y_count = mod_count // 2
    y, x = m // 2, m % 2
    partner = f + 1 - 2 * core
    steps = 2 * mod_count
    cycles = 2 * mod_count
    rows, per_cycle = packed.shape[1:]

    has_up1, has_up2 = chip + 1 < chips, chip + 2 < chips
    has_dn1, has_dn2 = chip >= 1, chip >= 2

    own, down1, down2, up1, up2 = 4 + core, 6 + core, 8 + core, 2 + core, core
    other_down1, other_down2, other_own = 7 - core, 9 - core, 5 - core

    loads = [
        pltpu.make_async_copy(src, dst, in_sem.at[i])
        for i, (src, dst) in enumerate(
            ((label_hbm, label), (good_hbm, good), (frames_hbm, frames))
        )
    ]
    for load in loads:
        load.start()

    def peer(o, sign):
        dy, dx = o // 2, o % 2
        return ((y + sign * dy + y_count) % y_count) * 2 + (x + dx) % 2

    barrier = pltpu.get_barrier_semaphore()

    def greet(cond, fr, mo):
        @pl.when(cond)
        def _():
            pl.semaphore_signal(barrier, inc=1, device_id=(fr, mo), device_id_type=MESH)

    for o in range(1, mod_count):
        pl.semaphore_signal(barrier, inc=1, device_id=(f, peer(o, 1)), device_id_type=MESH)
    pl.semaphore_signal(barrier, inc=1, device_id=(partner, m), device_id_type=MESH)
    greet(has_up1, f + 2, m)
    greet(has_up2, f + 4, m)
    greet(has_dn1, f - 2, m)
    greet(has_dn2, f - 4, m)
    arrivals = mod_count
    for cond in (has_up1, has_up2, has_dn1, has_dn2):
        arrivals = arrivals + jnp.where(cond, 1, 0)

    loads[0].wait()
    loads[1].wait()
    rank_pixels(label, good, place, partial, cycles, per_cycle)
    loads[2].wait()
    pl.semaphore_wait(barrier, arrivals)

    def remote(src, dst, send, recv, fr, mo):
        return pltpu.make_async_remote_copy(
            src_ref=src, dst_ref=dst, send_sem=send, recv_sem=recv,
            device_id=(fr, mo), device_id_type=MESH,
        )

    def forward(from_slot, to_slot, k, lane, fr):
        remote(
            held.at[from_slot, k], held.at[to_slot, k], send_sem.at[lane],
            recv_sem.at[to_slot, k], fr, m,
        ).start()

    def arrived(slot, k):
        pltpu.make_async_copy(held.at[slot, k], held.at[slot, k], recv_sem.at[slot, k]).wait()

    def arrange(k):
        cyc, o = k // mod_count, k % mod_count
        cycle = 2 * peer(o, -1) + cyc
        lane = lax.broadcasted_iota(jnp.int32, (256, 128), 1) + cycle * per_cycle
        wanted = [(lane + h * 128).astype(jnp.float32) for h in range(per_cycle // 128)]
        total = None
        for r in range(0, frames.shape[1], 256):
            spot = place[r : r + 256, :]
            hot = jnp.concatenate(
                [jnp.where(spot == w, 1.0, 0.0).astype(jnp.bfloat16) for w in wanted], axis=1
            )
            term = jnp.dot(frames[:, r : r + 256], hot, preferred_element_type=jnp.float32)
            total = term if total is None else total + term
        packed[k] = total.astype(jnp.bfloat16)

    def launch(k):
        o = k % mod_count

        @pl.when(o == 0)
        def _():
            pltpu.make_async_copy(packed.at[k], held.at[own, k], recv_sem.at[own, k]).start()

        @pl.when(o > 0)
        def _():
            remote(
                packed.at[k], held.at[own, k], send_sem.at[0], recv_sem.at[own, k], f, peer(o, -1)
            ).start()

    def own_stage(k):
        arrived(own, k)

        @pl.when(has_dn1)
        def _():
            forward(own, down1, k, 1, f - 2)

        @pl.when(has_up1)
        def _():
            forward(own, up1, k, 2, f + 2)

        forward(own, own, k, 3, partner)

    def relay_stage(k):
        @pl.when(has_up1)
        def _():
            arrived(down1, k)

            @pl.when(has_dn1)
            def _():
                forward(down1, down2, k, 4, f - 2)

            forward(down1, down1, k, 5, partner)

        @pl.when(has_dn1)
        def _():
            arrived(up1, k)

            @pl.when(has_up1)
            def _():
                forward(up1, up2, k, 6, f + 2)

    def share_stage(k):
        @pl.when(has_up2)
        def _():
            arrived(down2, k)
            forward(down2, down2, k, 7, partner)

    @pl.loop(0, mod_count + 1)
    def _(o):
        @pl.when(o < mod_count)
        def _():
            arrange(o)

        @pl.when(o >= 1)
        def _():
            launch(o - 1)

        @pl.when(o == 2)
        def _():
            own_stage(0)

    for o in range(mod_count):
        to = peer(o, -1)
        if o == 0:
            pltpu.make_async_copy(partial.at[to], counts.at[o], count_recv.at[o]).start()
        else:
            remote(partial.at[to], counts.at[o], count_send.at[o], count_recv.at[o], f, to).start()

    def step(k):
        @pl.when((k >= 1) & (k < steps))
        def _():
            own_stage(k)

        @pl.when(k < mod_count)
        def _():
            arrange(mod_count + k)

        @pl.when((k >= 1) & (k <= mod_count))
        def _():
            launch(mod_count + k - 1)

        @pl.when((k >= RELAY_LAG) & (k < steps + RELAY_LAG))
        def _():
            relay_stage(k - RELAY_LAG)

        @pl.when((k >= SHARE_LAG) & (k < steps + SHARE_LAG))
        def _():
            share_stage(k - SHARE_LAG)

    def far3_copy(cyc):
        return remote(
            far.at[cyc, pl.ds(0, 2)], tiles.at[cyc, pl.ds(6, 2)],
            far_send.at[cyc, 0], far_recv.at[cyc, 0], f - 2, m,
        )

    def far4_copy(cyc, i):
        return remote(
            far.at[cyc, 2 + i], tiles.at[cyc, 8 + i],
            far_send.at[cyc, 1 + i], far_recv.at[cyc, 1 + i], f - 4, m,
        )

    sends3, sends4 = has_dn1 & has_up2, has_dn2 & has_up2

    def compute(cyc):
        @pl.loop(0, mod_count)
        def _(o):
            k = cyc * mod_count + o
            arrived(other_own, k)

            @pl.when(has_up1)
            def _():
                arrived(other_down1, k)

            @pl.when(has_up2)
            def _():
                arrived(other_down2, k)

            @pl.when(has_dn2)
            def _():
                arrived(up2, k)

        count = counts[0]
        for o in range(1, mod_count):
            count = count + counts[o]
        count = count[cyc : cyc + 1]
        ones = jnp.ones((16, per_cycle), jnp.bfloat16)

        def products(lhs_slots, rhs_slot):
            total = None
            for o in range(mod_count):
                k = cyc * mod_count + o
                lhs = jnp.concatenate([held[s, k] for s in lhs_slots] + [ones], axis=0)
                rhs = held[rhs_slot : rhs_slot + 2, k].reshape(2 * rows, per_cycle)
                term = nt_dot(lhs, rhs)
                total = term if total is None else total + term
            return total

        def row_sums(slot):
            total = None
            for o in range(mod_count):
                block = held[slot, cyc * mod_count + o].astype(jnp.float32)
                total = block if total is None else total + block
            return jnp.sum(total, axis=1, keepdims=True)

        def tile(total, i, earlier, later, half):
            span = slice(half * 128, half * 128 + 128)
            return total[i * 128 : i * 128 + 128, span] * count / (earlier * later[:, span])

        mine = row_sums(own)

        @pl.when(has_up2)
        def _():
            total = products((up1, up2, own), 8)
            later = total[3 * rows : 3 * rows + 1]
            first, second = row_sums(up1), row_sums(up2)
            for half in range(2):
                far[cyc, half] = tile(total, 0, first, later, half)
                far[cyc, 2 + half] = tile(total, 1, second, later, half)
            for half in range(2):
                tiles[cyc, 4 + half] = tile(total, 2, mine, later, half)

        @pl.when(sends4)
        def _():
            far4_copy(cyc, 0).start()

            @pl.when(core == 1)
            def _():
                far4_copy(cyc, 1).start()

        @pl.when(sends3)
        def _():
            far3_copy(cyc).start()

        @pl.when(jnp.logical_not(has_up2))
        def _():
            tiles[cyc, 4:6] = jnp.zeros((2, 128, 128), jnp.float32)

        def near(rhs_slot):
            total = products((own,), rhs_slot)
            for half in range(2):
                tiles[cyc, rhs_slot - 4 + half] = tile(
                    total, 0, mine, total[rows : rows + 1], half
                )

        near(4)

        @pl.when(has_up1)
        def _():
            near(6)

        @pl.when(jnp.logical_not(has_up1))
        def _():
            tiles[cyc, 2:4] = jnp.zeros((2, 128, 128), jnp.float32)

    def out_copy(cyc):
        return pltpu.make_async_copy(out.at[cyc], out_hbm.at[cyc], out_sem.at[cyc])

    def finish(cyc):
        @pl.when(chip + 3 < chips)
        def _():
            far3_copy(cyc).wait_recv()

        @pl.when(chip + 3 >= chips)
        def _():
            tiles[cyc, 6:8] = jnp.zeros((2, 128, 128), jnp.float32)

        @pl.when(chip + 4 < chips)
        def _():
            far4_copy(cyc, 0).wait_recv()

            @pl.when(core == 1)
            def _():
                far4_copy(cyc, 1).wait_recv()

        @pl.when(chip + 4 >= chips)
        def _():
            tiles[cyc, 8:10] = jnp.zeros((2, 128, 128), jnp.float32)

        row = lax.broadcasted_iota(jnp.int32, (128, 128), 0)
        lane = lax.broadcasted_iota(jnp.int32, (128, 128), 1)
        inside = lane + row < 128

        def turned(j):
            piece = tiles[cyc, core + j]
            for bit in (1, 2, 4):
                piece = jnp.where(row // bit % 2 == 1, pltpu.roll(piece, 128 - bit, 1), piece)
            return jnp.concatenate(
                [piece[:8]] + [pltpu.roll(piece[r : r + 8], 128 - r, 1) for r in range(8, 128, 8)],
                axis=0,
            )

        now = turned(0)
        for j in range(LAG // 128):
            later = turned(j + 1)
            out[cyc, :, j * 128 : j * 128 + 128] = jnp.where(inside, now, later)
            now = later
        out_copy(cyc).start()

    middle = mod_count + FIRST_GRAM

    @pl.loop(0, middle)
    def _(k):
        step(k)

    for o in range(mod_count):
        pltpu.make_async_copy(counts.at[o], counts.at[o], count_recv.at[o]).wait()
    compute(0)

    @pl.loop(middle, steps + SHARE_LAG)
    def _(k):
        step(k)

    finish(0)
    compute(1)
    finish(1)

    def sent(lane, slot):
        pltpu.make_async_copy(held.at[slot], held.at[slot], send_sem.at[lane]).wait()

    for cyc in range(2):
        part = held.at[own, pl.ds(cyc * mod_count + 1, mod_count - 1)]
        pltpu.make_async_copy(part, part, send_sem.at[0]).wait()
    for o in range(1, mod_count):
        pltpu.make_async_copy(counts.at[o], counts.at[o], count_send.at[o]).wait()
    for lane, slot, cond in (
        (1, own, has_dn1), (2, own, has_up1), (3, own, None), (4, down1, has_up1 & has_dn1),
        (5, down1, has_up1), (6, up1, has_up1 & has_dn1), (7, down2, has_up2),
    ):
        if cond is None:
            sent(lane, slot)
        else:
            pl.when(cond)(functools.partial(sent, lane, slot))
    for cyc in range(2):
        @pl.when(sends3)
        def _():
            far3_copy(cyc).wait_send()

        @pl.when(sends4)
        def _():
            far4_copy(cyc, 0).wait_send()

            @pl.when(core == 1)
            def _():
                far4_copy(cyc, 1).wait_send()
        out_copy(cyc).wait()


def shards(frames, cycle_label, good_pixel):
    frame_count, mod_count = lax.axis_size("frame"), lax.axis_size("mod")
    rows, pixels = frames.shape
    steps = 2 * mod_count
    per_cycle = pixels // steps
    small = (pixels // 128, 128)
    return pl.pallas_call(
        functools.partial(kernel, frame_count, mod_count),
        out_shape=jax.ShapeDtypeStruct((2, rows, LAG), jnp.float32),
        in_specs=[pl.BlockSpec(memory_space=pl.ANY)] * 3,
        out_specs=pl.BlockSpec(memory_space=pl.ANY),
        scratch_shapes=[
            pltpu.VMEM((rows, pixels), jnp.bfloat16),
            pltpu.VMEM(small, jnp.int32),
            pltpu.VMEM(small, jnp.int32),
            pltpu.VMEM((pixels, 128), jnp.float32),
            pltpu.VMEM((mod_count, 8, 128), jnp.float32),
            pltpu.VMEM((steps, rows, per_cycle), jnp.bfloat16),
            pltpu.VMEM((10, steps, rows, per_cycle), jnp.bfloat16),
            pltpu.VMEM((mod_count, 8, 128), jnp.float32),
            pltpu.VMEM((2, 10, 128, 128), jnp.float32),
            pltpu.VMEM((2, 4, 128, 128), jnp.float32),
            pltpu.VMEM((2, rows, LAG), jnp.float32),
            pltpu.SemaphoreType.DMA((3,)),
            pltpu.SemaphoreType.DMA((2,)),
            pltpu.SemaphoreType.DMA((10, steps)),
            pltpu.SemaphoreType.DMA((8,)),
            pltpu.SemaphoreType.DMA((mod_count,)),
            pltpu.SemaphoreType.DMA((mod_count,)),
            pltpu.SemaphoreType.DMA((2, 3)),
            pltpu.SemaphoreType.DMA((2, 3)),
        ],
        compiler_params=pltpu.CompilerParams(
            collective_id=0, has_side_effects=True, vmem_limit_bytes=60 * 1024 * 1024
        ),
    )(frames, cycle_label.reshape(small), good_pixel.reshape(small))


def solution(mesh):
    placed = (P("frame", "mod"), P("mod"), P("mod"))
    return jax.shard_map(
        shards, mesh=mesh, in_specs=placed, out_specs=P("mod", "frame", None), check_vma=False
    )
```

time: 617 us -> 110 us (0.18)
  the two profiles are of different devices: /device:TPU:1 before, /device:TPU:66 now
where the time goes in v2:
time: 110 us
  Pallas kernels  108 us (98%)
  local copies, waits for them, and re-layouts  2.31 us (2%)
    pallas_call x1, Pallas kernels, shards(): pl.pallas_call(functools.partial(kernel, frame_count, mod_count), out_sha...  108 us
    unnamed x1, local copies, waits for them, and re-layouts  2.31 us

profile of v2, /device:TPU:66, one launch (start us, length us, event | category | flops | bytes accessed | tf_op | source)
XLA Modules:
  0.0 110.0 jit_solution(3836629117204673613)
XLA Ops:
  0.0 107.7 %shard_map.37 = f32[2,128,1024]{2,1,0:T(8,128)} custom-call(bf16[128,4096]{1,0:T(8,128)(2,1)} %frames_hbm.1, s32[32,128]{1,0:T(8,128)} %bitcast.2, s32[32,128]{1,0:T(8,128)} %bitcast.3), custom_call_target="tpu_custom_call" | custom-call | tf_op jit(solution)/shard_map/pallas_call | solution.py:443
  107.7 2.3 %copy.5 = f32[2,128,1024]{2,1,0:T(8,128)} copy(f32[2,128,1024]{2,1,0:T(8,128)} %shard_map.37) | data formatting | bytes 2097152

commit v3 on v2

--- a/solution.py
+++ b/solution.py
@@ -11,9 +11,6 @@
 LAG = 1024
 MESH = pl.DeviceIdType.MESH
 NT = (((1,), (1,)), ((), ()))
-RELAY_LAG = 3
-SHARE_LAG = 6
-FIRST_GRAM = 7
 
 
 def nt_dot(a, b):
@@ -54,9 +51,9 @@
 
 
 def kernel(
-    frame_count, mod_count, frames_hbm, label_hbm, good_hbm, out_hbm,
-    frames, label, good, place, partial, packed, held, counts, tiles, far, out,
-    in_sem, out_sem, recv_sem, send_sem, count_send, count_recv, far_send, far_recv,
+    frame_count, mod_count, frames_hbm, label_hbm, good_hbm, out,
+    frames, label, good, place, partial, packed, held, counts, tiles, far,
+    in_sem, recv_sem, send_sem, count_send, count_recv, far_send, far_recv,
 ):
     f = lax.axis_index("frame")
     m = lax.axis_index("mod")
@@ -215,26 +212,21 @@
         else:
             remote(partial.at[to], counts.at[o], count_send.at[o], count_recv.at[o], f, to).start()
 
-    def step(k):
-        @pl.when((k >= 1) & (k < steps))
-        def _():
-            own_stage(k)
-
-        @pl.when(k < mod_count)
-        def _():
-            arrange(mod_count + k)
-
-        @pl.when((k >= 1) & (k <= mod_count))
-        def _():
-            launch(mod_count + k - 1)
-
-        @pl.when((k >= RELAY_LAG) & (k < steps + RELAY_LAG))
-        def _():
-            relay_stage(k - RELAY_LAG)
-
-        @pl.when((k >= SHARE_LAG) & (k < steps + SHARE_LAG))
-        def _():
-            share_stage(k - SHARE_LAG)
+    @pl.loop(1, steps)
+    def _(k):
+        own_stage(k)
+
+        @pl.when(k <= mod_count)
+        def _():
+            arrange(mod_count + k - 1)
+
+        @pl.when((k >= 2) & (k <= mod_count + 1))
+        def _():
+            launch(mod_count + k - 2)
+
+    @pl.loop(0, steps)
+    def _(k):
+        relay_stage(k)
 
     def far3_copy(cyc):
         return remote(
@@ -341,9 +333,6 @@
         def _():
             tiles[cyc, 2:4] = jnp.zeros((2, 128, 128), jnp.float32)
 
-    def out_copy(cyc):
-        return pltpu.make_async_copy(out.at[cyc], out_hbm.at[cyc], out_sem.at[cyc])
-
     def finish(cyc):
         @pl.when(chip + 3 < chips)
         def _():
@@ -383,21 +372,18 @@
             later = turned(j + 1)
             out[cyc, :, j * 128 : j * 128 + 128] = jnp.where(inside, now, later)
             now = later
-        out_copy(cyc).start()
-
-    middle = mod_count + FIRST_GRAM
-
-    @pl.loop(0, middle)
+
+    @pl.loop(0, mod_count)
     def _(k):
-        step(k)
+        share_stage(k)
 
     for o in range(mod_count):
         pltpu.make_async_copy(counts.at[o], counts.at[o], count_recv.at[o]).wait()
     compute(0)
 
-    @pl.loop(middle, steps + SHARE_LAG)
+    @pl.loop(mod_count, steps)
     def _(k):
-        step(k)
+        share_stage(k)
 
     finish(0)
     compute(1)
@@ -431,7 +417,6 @@
             @pl.when(core == 1)
             def _():
                 far4_copy(cyc, 1).wait_send()
-        out_copy(cyc).wait()
 
 
 def shards(frames, cycle_label, good_pixel):
@@ -444,7 +429,7 @@
         functools.partial(kernel, frame_count, mod_count),
         out_shape=jax.ShapeDtypeStruct((2, rows, LAG), jnp.float32),
         in_specs=[pl.BlockSpec(memory_space=pl.ANY)] * 3,
-        out_specs=pl.BlockSpec(memory_space=pl.ANY),
+        out_specs=pl.BlockSpec(memory_space=pltpu.VMEM),
         scratch_shapes=[
             pltpu.VMEM((rows, pixels), jnp.bfloat16),
             pltpu.VMEM(small, jnp.int32),
@@ -456,9 +441,7 @@
             pltpu.VMEM((mod_count, 8, 128), jnp.float32),
             pltpu.VMEM((2, 10, 128, 128), jnp.float32),
             pltpu.VMEM((2, 4, 128, 128), jnp.float32),
-            pltpu.VMEM((2, rows, LAG), jnp.float32),
             pltpu.SemaphoreType.DMA((3,)),
-            pltpu.SemaphoreType.DMA((2,)),
             pltpu.SemaphoreType.DMA((10, steps)),
             pltpu.SemaphoreType.DMA((8,)),
             pltpu.SemaphoreType.DMA((mod_count,)),
@@ -467,7 +450,7 @@
             pltpu.SemaphoreType.DMA((2, 3)),
         ],
         compiler_params=pltpu.CompilerParams(
-            collective_id=0, has_side_effects=True, vmem_limit_bytes=60 * 1024 * 1024
+            collective_id=0, has_side_effects=True, vmem_limit_bytes=32 * 1024 * 1024
         ),
     )(frames, cycle_label.reshape(small), good_pixel.reshape(small))
 

time: 110 us -> 102 us (0.927)
  the two profiles are of different devices: /device:TPU:66 before, /device:TPU:99 now
where the time goes in v3:
time: 102 us
  Pallas kernels  98.6 us (97%)
  local copies, waits for them, and re-layouts  3.63 us (4%)
    pallas_call x1, Pallas kernels, shards(): pl.pallas_call(functools.partial(kernel, frame_count, mod_count), out_sha...  98.6 us
    unnamed x7, local copies, waits for them, and re-layouts  3.63 us

profile of v3, /device:TPU:99, one launch (start us, length us, event | category | flops | bytes accessed | tf_op | source)
XLA Modules:
  0.0 102.2 jit_solution(4487632272384502904)
XLA Ops:
  0.0 0.0 copy-start
  0.0 1.2 %copy-done = bf16[128,4096]{1,0:T(8,128)(2,1)S(1)} copy-done((bf16[128,4096]{1,0:T(8,128)(2,1)S(1)}, bf16[128,4096]{1,0:T(8,128)(2,1)}, u32[]{:S(2)}) %copy-start) | copy-done | bytes 1048600
  1.2 0.0 copy-start.1
  1.2 0.7 copy-done.1
  1.9 0.0 copy-start.2
  1.9 0.7 copy-done.2
  2.7 98.6 %shard_map.37 = f32[2,128,1024]{2,1,0:T(8,128)S(1)} custom-call(bf16[128,4096]{1,0:T(8,128)(2,1)S(1)} %copy-done, s32[32,128]{1,0:T(8,128)S(1)} %bitcast.2, s32[32,128]{1,0:T(8,128)S(1)} %bitcast.3), custom_call_target="tpu_custom_call" | custom-call | tf_op jit(solution)/shard_map/pallas_call | solution.py:428
  101.2 1.0 copy.5
Async XLA Ops:
  0.0 1.2 %copy-start = (bf16[128,4096]{1,0:T(8,128)(2,1)S(1)}, bf16[128,4096]{1,0:T(8,128)(2,1)}, u32[]{:S(2)}) copy-start(bf16[128,4096]{1,0:T(8,128)(2,1)} %frames_hbm.1) | copy-start | bytes 3145732
  1.2 0.7 copy-start.1
  1.9 0.7 copy-start.2

commit v4 on v3

--- a/solution.py
+++ b/solution.py
@@ -10,6 +10,7 @@
 CYCLES = 16
 LAG = 1024
 MESH = pl.DeviceIdType.MESH
+TRANSIT_LAG = 2
 NT = (((1,), (1,)), ((), ()))
 
 
@@ -82,6 +83,12 @@
     for load in loads:
         load.start()
 
+    half = chips // 2
+    first, last = chip == 0, chip == chips - 1
+    below, above = chip == half - 1, chip == half
+    at_first, at_last = core, frame_count - 2 + core
+    at_below, at_above = 2 * half - 2 + core, 2 * half + core
+
     def peer(o, sign):
         dy, dx = o // 2, o % 2
         return ((y + sign * dy + y_count) % y_count) * 2 + (x + dx) % 2
@@ -100,8 +107,14 @@
     greet(has_up2, f + 4, m)
     greet(has_dn1, f - 2, m)
     greet(has_dn2, f - 4, m)
+    for ends, targets in (
+        (first | last, (at_below, at_above)), (below | above, (at_first, at_last))
+    ):
+        for target in targets:
+            greet(ends, target, m)
     arrivals = mod_count
-    for cond in (has_up1, has_up2, has_dn1, has_dn2):
+    ends = first | last | below | above
+    for cond in (has_up1, has_up2, has_dn1, has_dn2, ends, ends):
         arrivals = arrivals + jnp.where(cond, 1, 0)
 
     loads[0].wait()
@@ -153,37 +166,56 @@
                 packed.at[k], held.at[own, k], send_sem.at[0], recv_sem.at[own, k], f, peer(o, -1)
             ).start()
 
+    def forward_down(from_slot, to_slot, by_slot, k, lane):
+        detour = above & (k % 2 == 1)
+
+        @pl.when(detour)
+        def _():
+            forward(from_slot, by_slot, k, lane, at_first)
+
+        @pl.when(has_dn1 & jnp.logical_not(detour))
+        def _():
+            forward(from_slot, to_slot, k, lane, f - 2)
+
+    def forward_up(from_slot, to_slot, by_slot, k, lane):
+        detour = below & (k % 2 == 1)
+
+        @pl.when(detour)
+        def _():
+            forward(from_slot, by_slot, k, lane, at_last)
+
+        @pl.when(has_up1 & jnp.logical_not(detour))
+        def _():
+            forward(from_slot, to_slot, k, lane, f + 2)
+
+    def transit(up_slot, down_slot, k, lane):
+        @pl.when(first)
+        def _():
+            arrived(up_slot, k)
+            forward(up_slot, down_slot, k, lane, at_below)
+
+        @pl.when(last)
+        def _():
+            arrived(down_slot, k)
+            forward(down_slot, up_slot, k, lane, at_above)
+
     def own_stage(k):
         arrived(own, k)
-
-        @pl.when(has_dn1)
-        def _():
-            forward(own, down1, k, 1, f - 2)
-
-        @pl.when(has_up1)
-        def _():
-            forward(own, up1, k, 2, f + 2)
-
+        forward_down(own, down1, up1, k, 1)
+        forward_up(own, up1, down1, k, 2)
         forward(own, own, k, 3, partner)
 
     def relay_stage(k):
         @pl.when(has_up1)
         def _():
             arrived(down1, k)
-
-            @pl.when(has_dn1)
-            def _():
-                forward(down1, down2, k, 4, f - 2)
-
+            forward_down(down1, down2, up2, k, 4)
             forward(down1, down1, k, 5, partner)
 
         @pl.when(has_dn1)
         def _():
             arrived(up1, k)
-
-            @pl.when(has_up1)
-            def _():
-                forward(up1, up2, k, 6, f + 2)
+            forward_up(up1, up2, down2, k, 6)
 
     def share_stage(k):
         @pl.when(has_up2)
@@ -224,9 +256,21 @@
         def _():
             launch(mod_count + k - 2)
 
+        @pl.when((k > TRANSIT_LAG) & (k % 2 == 1))
+        def _():
+            transit(up1, down1, k - TRANSIT_LAG, 8)
+
     @pl.loop(0, steps)
     def _(k):
         relay_stage(k)
+
+        @pl.when((k < TRANSIT_LAG) & (k % 2 == 1))
+        def _():
+            transit(up1, down1, steps - TRANSIT_LAG + k, 8)
+
+        @pl.when((k > TRANSIT_LAG) & (k % 2 == 1))
+        def _():
+            transit(up2, down2, k - TRANSIT_LAG, 9)
 
     def far3_copy(cyc):
         return remote(
@@ -375,6 +419,10 @@
 
     @pl.loop(0, mod_count)
     def _(k):
+        @pl.when((k < TRANSIT_LAG) & (k % 2 == 1))
+        def _():
+            transit(up2, down2, steps - TRANSIT_LAG + k, 9)
+
         share_stage(k)
 
     for o in range(mod_count):
@@ -391,6 +439,15 @@
 
     def sent(lane, slot):
         pltpu.make_async_copy(held.at[slot], held.at[slot], send_sem.at[lane]).wait()
+
+    def sent_half(lane, slot):
+        part = held.at[slot, pl.ds(0, mod_count)]
+        pltpu.make_async_copy(part, part, send_sem.at[lane]).wait()
+
+    @pl.when(first | last)
+    def _():
+        sent_half(8, up1)
+        sent_half(9, up2)
 
     for cyc in range(2):
         part = held.at[own, pl.ds(cyc * mod_count + 1, mod_count - 1)]
@@ -443,7 +500,7 @@
             pltpu.VMEM((2, 4, 128, 128), jnp.float32),
             pltpu.SemaphoreType.DMA((3,)),
             pltpu.SemaphoreType.DMA((10, steps)),
-            pltpu.SemaphoreType.DMA((8,)),
+            pltpu.SemaphoreType.DMA((10,)),
             pltpu.SemaphoreType.DMA((mod_count,)),
             pltpu.SemaphoreType.DMA((mod_count,)),
             pltpu.SemaphoreType.DMA((2, 3)),

time: 102 us -> 83.5 us (0.82)
  the two profiles are of different devices: /device:TPU:99 before, /device:TPU:1 now
where the time goes in v4:
time: 83.5 us; the launch traced here: 82.1 us
  Pallas kernels  78.4 us (94%)
  local copies, waits for them, and re-layouts  3.63 us (4%)
    pallas_call x1, Pallas kernels, shards(): pl.pallas_call(functools.partial(kernel, frame_count, mod_count), out_sha...  78.4 us
    unnamed x7, local copies, waits for them, and re-layouts  3.63 us

profile of v4, /device:TPU:1, one launch (start us, length us, event | category | flops | bytes accessed | tf_op | source)
XLA Modules:
  0.0 82.1 jit_solution(5870675724585952452)
XLA Ops:
  0.0 0.0 copy-start
  0.0 1.2 %copy-done = bf16[128,4096]{1,0:T(8,128)(2,1)S(1)} copy-done((bf16[128,4096]{1,0:T(8,128)(2,1)S(1)}, bf16[128,4096]{1,0:T(8,128)(2,1)}, u32[]{:S(2)}) %copy-start) | copy-done | bytes 1048600
  1.2 0.0 copy-start.1
  1.2 0.7 copy-done.1
  1.9 0.0 copy-start.2
  1.9 0.7 copy-done.2
  2.7 78.4 %shard_map.37 = f32[2,128,1024]{2,1,0:T(8,128)S(1)} custom-call(bf16[128,4096]{1,0:T(8,128)(2,1)S(1)} %copy-done, s32[32,128]{1,0:T(8,128)S(1)} %bitcast.2, s32[32,128]{1,0:T(8,128)S(1)} %bitcast.3), custom_call_target="tpu_custom_call" | custom-call | tf_op jit(solution)/shard_map/pallas_call | solution.py:485
  81.1 1.0 %copy.5 = f32[2,128,1024]{2,1,0:T(8,128)} copy(f32[2,128,1024]{2,1,0:T(8,128)S(1)} %shard_map.37) | data formatting | bytes 2097152
Async XLA Ops:
  0.0 1.2 %copy-start = (bf16[128,4096]{1,0:T(8,128)(2,1)S(1)}, bf16[128,4096]{1,0:T(8,128)(2,1)}, u32[]{:S(2)}) copy-start(bf16[128,4096]{1,0:T(8,128)(2,1)} %frames_hbm.1) | copy-start | bytes 3145732
  1.2 0.7 copy-start.1
  1.9 0.7 copy-start.2

commit v5 on v4

--- a/solution.py
+++ b/solution.py
@@ -11,6 +11,8 @@
 LAG = 1024
 MESH = pl.DeviceIdType.MESH
 TRANSIT_LAG = 2
+OWN_LAG = 6
+CODE = 5600.0
 NT = (((1,), (1,)), ((), ()))
 
 
@@ -53,7 +55,7 @@
 
 def kernel(
     frame_count, mod_count, frames_hbm, label_hbm, good_hbm, out,
-    frames, label, good, place, partial, packed, held, counts, tiles, far,
+    frames, label, good, place, partial, packed, held, counts, tiles, far, code,
     in_sem, recv_sem, send_sem, count_send, count_recv, far_send, far_recv,
 ):
     f = lax.axis_index("frame")
@@ -223,20 +225,6 @@
             arrived(down2, k)
             forward(down2, down2, k, 7, partner)
 
-    @pl.loop(0, mod_count + 1)
-    def _(o):
-        @pl.when(o < mod_count)
-        def _():
-            arrange(o)
-
-        @pl.when(o >= 1)
-        def _():
-            launch(o - 1)
-
-        @pl.when(o == 2)
-        def _():
-            own_stage(0)
-
     for o in range(mod_count):
         to = peer(o, -1)
         if o == 0:
@@ -244,43 +232,51 @@
         else:
             remote(partial.at[to], counts.at[o], count_send.at[o], count_recv.at[o], f, to).start()
 
-    @pl.loop(1, steps)
-    def _(k):
-        own_stage(k)
-
-        @pl.when(k <= mod_count)
-        def _():
-            arrange(mod_count + k - 1)
-
-        @pl.when((k >= 2) & (k <= mod_count + 1))
-        def _():
-            launch(mod_count + k - 2)
-
-        @pl.when((k > TRANSIT_LAG) & (k % 2 == 1))
-        def _():
-            transit(up1, down1, k - TRANSIT_LAG, 8)
+    def slab(i):
+        early = jnp.where(i == 1, mod_count, i - 1)
+        return jnp.where((i >= 1) & (i <= mod_count), early, i)
+
+    @pl.loop(0, steps + OWN_LAG + TRANSIT_LAG)
+    def _(i):
+        @pl.when(i < steps)
+        def _():
+            arrange(slab(i))
+
+        @pl.when((i >= 1) & (i <= steps))
+        def _():
+            launch(slab(i - 1))
+
+        @pl.when((i >= 2) & (i < 4))
+        def _():
+            own_stage(slab(i - 2))
+
+        @pl.when((i >= OWN_LAG + 2) & (i < steps + OWN_LAG))
+        def _():
+            own_stage(slab(i - OWN_LAG))
+
+        passed = slab(i - OWN_LAG - TRANSIT_LAG)
+
+        @pl.when((i >= OWN_LAG + TRANSIT_LAG) & (passed % 2 == 1))
+        def _():
+            transit(up1, down1, passed, 8)
 
     @pl.loop(0, steps)
     def _(k):
         relay_stage(k)
 
-        @pl.when((k < TRANSIT_LAG) & (k % 2 == 1))
-        def _():
-            transit(up1, down1, steps - TRANSIT_LAG + k, 8)
-
         @pl.when((k > TRANSIT_LAG) & (k % 2 == 1))
         def _():
             transit(up2, down2, k - TRANSIT_LAG, 9)
 
     def far3_copy(cyc):
         return remote(
-            far.at[cyc, pl.ds(0, 2)], tiles.at[cyc, pl.ds(6, 2)],
+            far.at[cyc, pl.ds(0, 2)], code.at[cyc, pl.ds(0, 2)],
             far_send.at[cyc, 0], far_recv.at[cyc, 0], f - 2, m,
         )
 
     def far4_copy(cyc, i):
         return remote(
-            far.at[cyc, 2 + i], tiles.at[cyc, 8 + i],
+            far.at[cyc, 2 + i], code.at[cyc, 2 + i],
             far_send.at[cyc, 1 + i], far_recv.at[cyc, 1 + i], f - 4, m,
         )
 
@@ -327,6 +323,9 @@
                 total = block if total is None else total + block
             return jnp.sum(total, axis=1, keepdims=True)
 
+        def coded(value):
+            return jnp.round(jnp.log(value) * CODE).astype(jnp.int32).astype(jnp.int16)
+
         def tile(total, i, earlier, later, half):
             span = slice(half * 128, half * 128 + 128)
             return total[i * 128 : i * 128 + 128, span] * count / (earlier * later[:, span])
@@ -339,8 +338,8 @@
             later = total[3 * rows : 3 * rows + 1]
             first, second = row_sums(up1), row_sums(up2)
             for half in range(2):
-                far[cyc, half] = tile(total, 0, first, later, half)
-                far[cyc, 2 + half] = tile(total, 1, second, later, half)
+                far[cyc, half] = coded(tile(total, 0, first, later, half))
+                far[cyc, 2 + half] = coded(tile(total, 1, second, later, half))
             for half in range(2):
                 tiles[cyc, 4 + half] = tile(total, 2, mine, later, half)
 
@@ -378,25 +377,38 @@
             tiles[cyc, 2:4] = jnp.zeros((2, 128, 128), jnp.float32)
 
     def finish(cyc):
+        def decode(i):
+            value = code[cyc, i].astype(jnp.int32).astype(jnp.float32)
+            tiles[cyc, 6 + i] = jnp.exp(value * (1.0 / CODE))
+
+        def clear(i):
+            tiles[cyc, 6 + i] = jnp.zeros((128, 128), jnp.float32)
+
         @pl.when(chip + 3 < chips)
         def _():
             far3_copy(cyc).wait_recv()
+            decode(0)
+            decode(1)
 
         @pl.when(chip + 3 >= chips)
         def _():
-            tiles[cyc, 6:8] = jnp.zeros((2, 128, 128), jnp.float32)
+            clear(0)
+            clear(1)
 
         @pl.when(chip + 4 < chips)
         def _():
             far4_copy(cyc, 0).wait_recv()
+            decode(2)
 
             @pl.when(core == 1)
             def _():
                 far4_copy(cyc, 1).wait_recv()
+                decode(3)
 
         @pl.when(chip + 4 >= chips)
         def _():
-            tiles[cyc, 8:10] = jnp.zeros((2, 128, 128), jnp.float32)
+            clear(2)
+            clear(3)
 
         row = lax.broadcasted_iota(jnp.int32, (128, 128), 0)
         lane = lax.broadcasted_iota(jnp.int32, (128, 128), 1)
@@ -497,7 +509,8 @@
             pltpu.VMEM((10, steps, rows, per_cycle), jnp.bfloat16),
             pltpu.VMEM((mod_count, 8, 128), jnp.float32),
             pltpu.VMEM((2, 10, 128, 128), jnp.float32),
-            pltpu.VMEM((2, 4, 128, 128), jnp.float32),
+            pltpu.VMEM((2, 4, 128, 128), jnp.int16),
+            pltpu.VMEM((2, 4, 128, 128), jnp.int16),
             pltpu.SemaphoreType.DMA((3,)),
             pltpu.SemaphoreType.DMA((10, steps)),
             pltpu.SemaphoreType.DMA((10,)),
@@ -509,7 +522,7 @@
         compiler_params=pltpu.CompilerParams(
             collective_id=0, has_side_effects=True, vmem_limit_bytes=32 * 1024 * 1024
         ),
-    )(frames, cycle_label.reshape(small), good_pixel.reshape(small))
+    )(pltpu.with_memory_space_constraint(frames, pltpu.HBM), cycle_label.reshape(small), good_pixel.reshape(small))
 
 
 def solution(mesh):

time: 83.5 us -> 75.1 us (0.90)
  the two profiles are of different devices: /device:TPU:1 before, /device:TPU:24 now
where the time goes in v5:
time: 75.1 us; the launch traced here: 74.8 us
  Pallas kernels  72.4 us (96%)
  local copies, waits for them, and re-layouts  2.41 us (3%)
    pallas_call x1, Pallas kernels, shards(): pl.pallas_call(functools.partial(kernel, frame_count, mod_count), out_sha...  72.4 us
    unnamed x5, local copies, waits for them, and re-layouts  2.41 us

profile of v5, /device:TPU:24, one launch (start us, length us, event | category | flops | bytes accessed | tf_op | source)
XLA Modules:
  0.0 74.8 jit_solution(15745391719251510920)
XLA Ops:
  0.0 0.0 copy-start
  0.0 0.7 copy-done
  0.7 0.0 copy-start.1
  0.7 0.7 copy-done.1
  1.4 72.4 %shard_map.37 = f32[2,128,1024]{2,1,0:T(8,128)S(1)} custom-call(bf16[128,4096]{1,0:T(8,128)(2,1)} %frames_hbm.1, s32[32,128]{1,0:T(8,128)S(1)} %bitcast.2, s32[32,128]{1,0:T(8,128)S(1)} %bitcast.3), custom_call_target="tpu_custom_call" | custom-call | tf_op jit(solution)/shard_map/pallas_call | solution.py:497
  73.8 1.0 %copy.5 = f32[2,128,1024]{2,1,0:T(8,128)} copy(f32[2,128,1024]{2,1,0:T(8,128)S(1)} %shard_map.37) | data formatting | bytes 2097152
Async XLA Ops:
  0.0 0.7 copy-start
  0.7 0.7 copy-start.1

commit v6 on v5

--- a/solution.py
+++ b/solution.py
@@ -12,6 +12,7 @@
 MESH = pl.DeviceIdType.MESH
 TRANSIT_LAG = 2
 OWN_LAG = 6
+RELAY_LAG = 6
 CODE = 5600.0
 NT = (((1,), (1,)), ((), ()))
 
@@ -32,18 +33,18 @@
     packed = member.astype(jnp.bfloat16)
     in_row = jnp.dot(packed, upper, preferred_element_type=jnp.float32)
     totals = jnp.dot(packed, ones, preferred_element_type=jnp.float32).astype(jnp.bfloat16)
-    size = cycles * rows
-    here = lax.broadcasted_iota(jnp.int32, (size, size), 0)
-    there = lax.broadcasted_iota(jnp.int32, (size, size), 1)
-    earlier = jnp.where((here // rows == there // rows) & (there < here), 1.0, 0.0)
-    above = jnp.dot(earlier.astype(jnp.bfloat16), totals, preferred_element_type=jnp.float32)
-    ranks = (in_row + above) * member
+    side = jnp.concatenate([totals[c * rows : (c + 1) * rows] for c in range(cycles)], axis=1)
+    here = lax.broadcasted_iota(jnp.int32, (rows, rows), 0)
+    there = lax.broadcasted_iota(jnp.int32, (rows, rows), 1)
+    earlier = jnp.where(there < here, 1.0, 0.0).astype(jnp.bfloat16)
+    above = jnp.dot(earlier, side, preferred_element_type=jnp.float32)
     usable = jnp.where(good, 1.0, 0.0)
     partial[...] = jnp.zeros_like(partial)
     total = None
     for c in range(cycles):
         mine = slice(c * rows, (c + 1) * rows)
-        total = ranks[mine] if total is None else total + ranks[mine]
+        ranks = (in_row[mine] + above[:, c * lanes : (c + 1) * lanes]) * member[mine]
+        total = ranks if total is None else total + ranks
         per_row = jnp.sum(member[mine] * usable, axis=0, keepdims=True)
         partial[c // 2, c % 2 : c % 2 + 1, :] = jnp.broadcast_to(
             jnp.sum(per_row, axis=1, keepdims=True), (1, lanes)
@@ -55,7 +56,7 @@
 
 def kernel(
     frame_count, mod_count, frames_hbm, label_hbm, good_hbm, out,
-    frames, label, good, place, partial, packed, held, counts, tiles, far, code,
+    frames, label, good, place, partial, packed, held, counts, tiles, far, code, gram, sums,
     in_sem, recv_sem, send_sem, count_send, count_recv, far_send, far_recv,
 ):
     f = lax.axis_index("frame")
@@ -132,8 +133,9 @@
         )
 
     def forward(from_slot, to_slot, k, lane, fr):
+        source = packed.at[k] if from_slot is None else held.at[from_slot, k]
         remote(
-            held.at[from_slot, k], held.at[to_slot, k], send_sem.at[lane],
+            source, held.at[to_slot, k], send_sem.at[lane],
             recv_sem.at[to_slot, k], fr, m,
         ).start()
 
@@ -201,11 +203,10 @@
             arrived(down_slot, k)
             forward(down_slot, up_slot, k, lane, at_above)
 
-    def own_stage(k):
-        arrived(own, k)
-        forward_down(own, down1, up1, k, 1)
-        forward_up(own, up1, down1, k, 2)
-        forward(own, own, k, 3, partner)
+    def own_stage(k, source):
+        forward_down(source, down1, up1, k, 1)
+        forward_up(source, up1, down1, k, 2)
+        forward(source, own, k, 3, partner)
 
     def relay_stage(k):
         @pl.when(has_up1)
@@ -236,7 +237,7 @@
         early = jnp.where(i == 1, mod_count, i - 1)
         return jnp.where((i >= 1) & (i <= mod_count), early, i)
 
-    @pl.loop(0, steps + OWN_LAG + TRANSIT_LAG)
+    @pl.loop(0, steps + OWN_LAG + RELAY_LAG + TRANSIT_LAG)
     def _(i):
         @pl.when(i < steps)
         def _():
@@ -246,27 +247,32 @@
         def _():
             launch(slab(i - 1))
 
-        @pl.when((i >= 2) & (i < 4))
-        def _():
-            own_stage(slab(i - 2))
+        @pl.when((i >= 1) & (i < 3))
+        def _():
+            own_stage(slab(i - 1), None)
 
         @pl.when((i >= OWN_LAG + 2) & (i < steps + OWN_LAG))
         def _():
-            own_stage(slab(i - OWN_LAG))
+            arrived(own, slab(i - OWN_LAG))
+            own_stage(slab(i - OWN_LAG), own)
 
         passed = slab(i - OWN_LAG - TRANSIT_LAG)
 
-        @pl.when((i >= OWN_LAG + TRANSIT_LAG) & (passed % 2 == 1))
+        @pl.when((i >= OWN_LAG + TRANSIT_LAG) & (passed < steps) & (passed % 2 == 1))
         def _():
             transit(up1, down1, passed, 8)
 
-    @pl.loop(0, steps)
-    def _(k):
-        relay_stage(k)
-
-        @pl.when((k > TRANSIT_LAG) & (k % 2 == 1))
-        def _():
-            transit(up2, down2, k - TRANSIT_LAG, 9)
+        relayed = i - OWN_LAG - RELAY_LAG
+
+        @pl.when((relayed >= 0) & (relayed < steps))
+        def _():
+            relay_stage(slab(relayed))
+
+        passed_on = slab(relayed - TRANSIT_LAG)
+
+        @pl.when((relayed >= TRANSIT_LAG) & (passed_on % 2 == 1))
+        def _():
+            transit(up2, down2, passed_on, 9)
 
     def far3_copy(cyc):
         return remote(
@@ -282,7 +288,37 @@
 
     sends3, sends4 = has_dn1 & has_up2, has_dn2 & has_up2
 
-    def compute(cyc):
+    everything = range(mod_count)
+
+    def products(cyc, lhs_slots, rhs_slot, span):
+        ones = jnp.ones((16, per_cycle), jnp.bfloat16)
+        total = None
+        for o in span:
+            k = cyc * mod_count + o
+            lhs = jnp.concatenate([held[s, k] for s in lhs_slots] + [ones], axis=0)
+            rhs = held[rhs_slot : rhs_slot + 2, k].reshape(2 * rows, per_cycle)
+            term = nt_dot(lhs, rhs)
+            total = term if total is None else total + term
+        return total
+
+    def row_sums(cyc, slot, span):
+        total = None
+        for o in span:
+            block = held[slot, cyc * mod_count + o].astype(jnp.float32)
+            total = block if total is None else total + block
+        return jnp.broadcast_to(jnp.sum(total, axis=1, keepdims=True), (rows, 128))
+
+    def cycle_count(cyc):
+        count = counts[0]
+        for o in range(1, mod_count):
+            count = count + counts[o]
+        return count[cyc : cyc + 1]
+
+    def correlated(total, i, earlier, later, side, count):
+        span = slice(side * 128, side * 128 + 128)
+        return total[i * 128 : i * 128 + 128, span] * count / (earlier * later[:, span])
+
+    def near(cyc):
         @pl.loop(0, mod_count)
         def _(o):
             k = cyc * mod_count + o
@@ -292,6 +328,39 @@
             def _():
                 arrived(other_down1, k)
 
+        arrived(own, cyc * mod_count)
+        count = cycle_count(cyc)
+        mine = row_sums(cyc, own, everything)
+        sums[cyc, 0] = mine
+
+        @pl.when(has_dn1)
+        def _():
+            sums[cyc, 1] = row_sums(cyc, up1, everything)
+
+        def part(rhs_slot):
+            total = products(cyc, (own,), rhs_slot, everything)
+            for side in range(2):
+                tiles[cyc, rhs_slot - 4 + side] = correlated(
+                    total, 0, mine, total[rows : rows + 1], side, count
+                )
+
+        part(4)
+
+        @pl.when(has_up1)
+        def _():
+            part(6)
+
+        @pl.when(jnp.logical_not(has_up1))
+        def _():
+            tiles[cyc, 2:4] = jnp.zeros((2, 128, 128), jnp.float32)
+
+        blocks(cyc, 0, 2)
+
+    def gather_far(cyc, start, stop):
+        @pl.loop(start, stop)
+        def _(o):
+            k = cyc * mod_count + o
+
             @pl.when(has_up2)
             def _():
                 arrived(other_down2, k)
@@ -300,48 +369,34 @@
             def _():
                 arrived(up2, k)
 
-        count = counts[0]
-        for o in range(1, mod_count):
-            count = count + counts[o]
-        count = count[cyc : cyc + 1]
-        ones = jnp.ones((16, per_cycle), jnp.bfloat16)
-
-        def products(lhs_slots, rhs_slot):
-            total = None
-            for o in range(mod_count):
-                k = cyc * mod_count + o
-                lhs = jnp.concatenate([held[s, k] for s in lhs_slots] + [ones], axis=0)
-                rhs = held[rhs_slot : rhs_slot + 2, k].reshape(2 * rows, per_cycle)
-                term = nt_dot(lhs, rhs)
-                total = term if total is None else total + term
-            return total
-
-        def row_sums(slot):
-            total = None
-            for o in range(mod_count):
-                block = held[slot, cyc * mod_count + o].astype(jnp.float32)
-                total = block if total is None else total + block
-            return jnp.sum(total, axis=1, keepdims=True)
-
-        def coded(value):
-            return jnp.round(jnp.log(value) * CODE).astype(jnp.int32).astype(jnp.int16)
-
-        def tile(total, i, earlier, later, half):
-            span = slice(half * 128, half * 128 + 128)
-            return total[i * 128 : i * 128 + 128, span] * count / (earlier * later[:, span])
-
-        mine = row_sums(own)
-
         @pl.when(has_up2)
         def _():
-            total = products((up1, up2, own), 8)
+            span = range(start, stop)
+            total = products(cyc, (up1, up2, own), 8, span)
+            second = row_sums(cyc, up2, span)
+            if start > 0:
+                total, second = total + gram[...], second + sums[cyc, 2]
+            gram[...] = total
+            sums[cyc, 2] = second
+
+    def far_tiles(cyc):
+        @pl.when(has_up2)
+        def _():
+            count = cycle_count(cyc)
+            total = gram[...]
             later = total[3 * rows : 3 * rows + 1]
-            first, second = row_sums(up1), row_sums(up2)
-            for half in range(2):
-                far[cyc, half] = coded(tile(total, 0, first, later, half))
-                far[cyc, 2 + half] = coded(tile(total, 1, second, later, half))
-            for half in range(2):
-                tiles[cyc, 4 + half] = tile(total, 2, mine, later, half)
+
+            def coded(i):
+                for side in range(2):
+                    value = correlated(total, i, sums[cyc, 1 + i], later, side, count)
+                    far[cyc, 2 * i + side] = (
+                        jnp.round(jnp.log(value) * CODE).astype(jnp.int32).astype(jnp.int16)
+                    )
+
+            coded(1)
+            coded(0)
+            for side in range(2):
+                tiles[cyc, 4 + side] = correlated(total, 2, sums[cyc, 0], later, side, count)
 
         @pl.when(sends4)
         def _():
@@ -358,23 +413,6 @@
         @pl.when(jnp.logical_not(has_up2))
         def _():
             tiles[cyc, 4:6] = jnp.zeros((2, 128, 128), jnp.float32)
-
-        def near(rhs_slot):
-            total = products((own,), rhs_slot)
-            for half in range(2):
-                tiles[cyc, rhs_slot - 4 + half] = tile(
-                    total, 0, mine, total[rows : rows + 1], half
-                )
-
-        near(4)
-
-        @pl.when(has_up1)
-        def _():
-            near(6)
-
-        @pl.when(jnp.logical_not(has_up1))
-        def _():
-            tiles[cyc, 2:4] = jnp.zeros((2, 128, 128), jnp.float32)
 
     def finish(cyc):
         def decode(i):
@@ -410,6 +448,9 @@
             clear(2)
             clear(3)
 
+        blocks(cyc, 2, LAG // 128)
+
+    def blocks(cyc, start, stop):
         row = lax.broadcasted_iota(jnp.int32, (128, 128), 0)
         lane = lax.broadcasted_iota(jnp.int32, (128, 128), 1)
         inside = lane + row < 128
@@ -423,30 +464,32 @@
                 axis=0,
             )
 
-        now = turned(0)
-        for j in range(LAG // 128):
+        now = turned(start)
+        for j in range(start, stop):
             later = turned(j + 1)
             out[cyc, :, j * 128 : j * 128 + 128] = jnp.where(inside, now, later)
             now = later
 
-    @pl.loop(0, mod_count)
-    def _(k):
-        @pl.when((k < TRANSIT_LAG) & (k % 2 == 1))
-        def _():
-            transit(up2, down2, steps - TRANSIT_LAG + k, 9)
-
-        share_stage(k)
-
     for o in range(mod_count):
         pltpu.make_async_copy(counts.at[o], counts.at[o], count_recv.at[o]).wait()
-    compute(0)
-
-    @pl.loop(mod_count, steps)
-    def _(k):
-        share_stage(k)
-
+    near(0)
+    near(1)
+
+    def share(start, stop):
+        @pl.loop(start, stop)
+        def _(k):
+            share_stage(k)
+
+    share(0, mod_count)
+    gather_far(0, 0, mod_count)
+    far_tiles(0)
+    split = max(1, mod_count - 2)
+    share(mod_count, mod_count + split)
+    gather_far(1, 0, split)
+    share(mod_count + split, steps)
+    gather_far(1, split, mod_count)
+    far_tiles(1)
     finish(0)
-    compute(1)
     finish(1)
 
     def sent(lane, slot):
@@ -511,6 +554,8 @@
             pltpu.VMEM((2, 10, 128, 128), jnp.float32),
             pltpu.VMEM((2, 4, 128, 128), jnp.int16),
             pltpu.VMEM((2, 4, 128, 128), jnp.int16),
+            pltpu.VMEM((3 * rows + 16, 256), jnp.float32),
+            pltpu.VMEM((2, 3, 128, 128), jnp.float32),
             pltpu.SemaphoreType.DMA((3,)),
             pltpu.SemaphoreType.DMA((10, steps)),
             pltpu.SemaphoreType.DMA((10,)),

time: 75.1 us -> 72.5 us (0.965)
  the two profiles are of different devices: /device:TPU:24 before, /device:TPU:1 now
where the time goes in v6:
time: 72.5 us; the launch traced here: 71.5 us
  Pallas kernels  69.1 us (95%)
  local copies, waits for them, and re-layouts  2.41 us (3%)
    pallas_call x1, Pallas kernels, shards(): pl.pallas_call(functools.partial(kernel, frame_count, mod_count), out_sha...  69.1 us
    unnamed x5, local copies, waits for them, and re-layouts  2.41 us

profile of v6, /device:TPU:1, one launch (start us, length us, event | category | flops | bytes accessed | tf_op | source)
XLA Modules:
  0.0 71.5 jit_solution(16431378853131935969)
XLA Ops:
  0.0 0.0 copy-start
  0.0 0.7 %copy-done = s32[4096]{0:T(1024)S(1)} copy-done((s32[4096]{0:T(1024)S(1)}, s32[4096]{0:T(1024)}, u32[]{:S(2)}) %copy-start) | copy-done | bytes 16408
  0.7 0.0 copy-start.1
  0.7 0.7 %copy-done.1 = s32[4096]{0:T(1024)S(1)} copy-done((s32[4096]{0:T(1024)S(1)}, s32[4096]{0:T(1024)}, u32[]{:S(2)}) %copy-start.1) | copy-done | bytes 16408
  1.4 69.1 %shard_map.37 = f32[2,128,1024]{2,1,0:T(8,128)S(1)} custom-call(bf16[128,4096]{1,0:T(8,128)(2,1)} %frames_hbm.1, s32[32,128]{1,0:T(8,128)S(1)} %bitcast.2, s32[32,128]{1,0:T(8,128)S(1)} %bitcast.3), custom_call_target="tpu_custom_call" | custom-call | tf_op jit(solution)/shard_map/pallas_call | solution.py:540
  70.5 1.0 %copy.5 = f32[2,128,1024]{2,1,0:T(8,128)} copy(f32[2,128,1024]{2,1,0:T(8,128)S(1)} %shard_map.37) | data formatting | bytes 2097152
Async XLA Ops:
  0.0 0.7 %copy-start = (s32[4096]{0:T(1024)S(1)}, s32[4096]{0:T(1024)}, u32[]{:S(2)}) copy-start(s32[4096]{0:T(1024)} %param.4) | copy-start | bytes 49156
  0.7 0.7 %copy-start.1 = (s32[4096]{0:T(1024)S(1)}, s32[4096]{0:T(1024)}, u32[]{:S(2)}) copy-start(s32[4096]{0:T(1024)} %param.5) | copy-start | bytes 49156

commit v7 on v6

--- a/solution.py
+++ b/solution.py
@@ -56,7 +56,7 @@
 
 def kernel(
     frame_count, mod_count, frames_hbm, label_hbm, good_hbm, out,
-    frames, label, good, place, partial, packed, held, counts, tiles, far, code, gram, sums,
+    frames, label, good, place, partial, packed, held, counts, tiles, far, code, corner, corner_code, gram, sums,
     in_sem, recv_sem, send_sem, count_send, count_recv, far_send, far_recv,
 ):
     f = lax.axis_index("frame")
@@ -281,10 +281,30 @@
         )
 
     def far4_copy(cyc, i):
+        source, target = (far, code) if i else (corner, corner_code)
+        place_of = (cyc, 2) if i else (cyc,)
         return remote(
-            far.at[cyc, 2 + i], code.at[cyc, 2 + i],
+            source.at[place_of], target.at[place_of],
             far_send.at[cyc, 1 + i], far_recv.at[cyc, 1 + i], f - 4, m,
         )
+
+    def folded(tile):
+        lane = lax.broadcasted_iota(jnp.int32, (8, 128), 1)
+        parts = [
+            jnp.where(
+                lane < 8 * g + 8,
+                tile[8 * g : 8 * g + 8],
+                pltpu.roll(tile[112 - 8 * g : 120 - 8 * g], 8 * g + 8, 1),
+            )
+            for g in range(8, 15)
+        ]
+        return jnp.concatenate(parts + [tile[120:], tile[56:64], tile[56:64]], axis=0)
+
+    def unfolded(tile):
+        parts = [
+            pltpu.roll(tile[8 * (6 - h) : 8 * (6 - h) + 8], 8 * h + 8, 1) for h in range(7)
+        ]
+        return jnp.concatenate(parts + [tile[64:72], tile[:56], tile[56:64]], axis=0)
 
     sends3, sends4 = has_dn1 & has_up2, has_dn2 & has_up2
 
@@ -386,15 +406,15 @@
             total = gram[...]
             later = total[3 * rows : 3 * rows + 1]
 
-            def coded(i):
-                for side in range(2):
-                    value = correlated(total, i, sums[cyc, 1 + i], later, side, count)
-                    far[cyc, 2 * i + side] = (
-                        jnp.round(jnp.log(value) * CODE).astype(jnp.int32).astype(jnp.int16)
-                    )
-
-            coded(1)
-            coded(0)
+            def coded(i, side):
+                value = correlated(total, i, sums[cyc, 1 + i], later, side, count)
+                return jnp.round(jnp.log(value) * CODE).astype(jnp.int32)
+
+            near_side, far_side = coded(1, 0), coded(1, 1)
+            far[cyc, 2] = near_side.astype(jnp.int16)
+            corner[cyc] = folded(jnp.where(core == 0, near_side, far_side)).astype(jnp.int16)
+            for side in range(2):
+                far[cyc, side] = coded(0, side).astype(jnp.int16)
             for side in range(2):
                 tiles[cyc, 4 + side] = correlated(total, 2, sums[cyc, 0], later, side, count)
 
@@ -436,12 +456,13 @@
         @pl.when(chip + 4 < chips)
         def _():
             far4_copy(cyc, 0).wait_recv()
-            decode(2)
+            value = unfolded(corner_code[cyc].astype(jnp.int32)).astype(jnp.float32)
+            tiles[cyc, 8 + core] = jnp.exp(value * (1.0 / CODE))
 
             @pl.when(core == 1)
             def _():
                 far4_copy(cyc, 1).wait_recv()
-                decode(3)
+                decode(2)
 
         @pl.when(chip + 4 >= chips)
         def _():
@@ -552,8 +573,10 @@
             pltpu.VMEM((10, steps, rows, per_cycle), jnp.bfloat16),
             pltpu.VMEM((mod_count, 8, 128), jnp.float32),
             pltpu.VMEM((2, 10, 128, 128), jnp.float32),
-            pltpu.VMEM((2, 4, 128, 128), jnp.int16),
-            pltpu.VMEM((2, 4, 128, 128), jnp.int16),
+            pltpu.VMEM((2, 3, 128, 128), jnp.int16),
+            pltpu.VMEM((2, 3, 128, 128), jnp.int16),
+            pltpu.VMEM((2, 80, 128), jnp.int16),
+            pltpu.VMEM((2, 80, 128), jnp.int16),
             pltpu.VMEM((3 * rows + 16, 256), jnp.float32),
             pltpu.VMEM((2, 3, 128, 128), jnp.float32),
             pltpu.SemaphoreType.DMA((3,)),

time: 72.5 us -> 71.9 us (level); the launches traced: 71.5 us -> 71.7 us
  no operation moved by 1% of the time
where the time goes in v7:
time: 71.9 us; the launch traced here: 71.7 us
  Pallas kernels  69.3 us (96%)
  local copies, waits for them, and re-layouts  2.41 us (3%)
    pallas_call x1, Pallas kernels, shards(): pl.pallas_call(functools.partial(kernel, frame_count, mod_count), out_sha...  69.3 us
    unnamed x5, local copies, waits for them, and re-layouts  2.41 us

profile of v7, /device:TPU:1, one launch (start us, length us, event | category | flops | bytes accessed | tf_op | source)
XLA Modules:
  0.0 71.7 jit_solution(2977848331778232111)
XLA Ops:
  0.0 0.0 copy-start
  0.0 0.7 copy-done
  0.7 0.0 copy-start.1
  0.7 0.7 copy-done.1
  1.4 69.3 %shard_map.37 = f32[2,128,1024]{2,1,0:T(8,128)S(1)} custom-call(bf16[128,4096]{1,0:T(8,128)(2,1)} %frames_hbm.1, s32[32,128]{1,0:T(8,128)S(1)} %bitcast.2, s32[32,128]{1,0:T(8,128)S(1)} %bitcast.3), custom_call_target="tpu_custom_call" | custom-call | tf_op jit(solution)/shard_map/pallas_call | solution.py:561
  70.7 1.0 %copy.5 = f32[2,128,1024]{2,1,0:T(8,128)} copy(f32[2,128,1024]{2,1,0:T(8,128)S(1)} %shard_map.37) | data formatting | bytes 2097152
Async XLA Ops:
  0.0 0.7 %copy-start = (s32[4096]{0:T(1024)S(1)}, s32[4096]{0:T(1024)}, u32[]{:S(2)}) copy-start(s32[4096]{0:T(1024)} %param.4) | copy-start | bytes 49156
  0.7 0.7 %copy-start.1 = (s32[4096]{0:T(1024)S(1)}, s32[4096]{0:T(1024)}, u32[]{:S(2)}) copy-start(s32[4096]{0:T(1024)} %param.5) | copy-start | bytes 49156

commit v8 on v7

--- a/solution.py
+++ b/solution.py
@@ -11,7 +11,7 @@
 LAG = 1024
 MESH = pl.DeviceIdType.MESH
 TRANSIT_LAG = 2
-OWN_LAG = 6
+OWN_LAG = 5
 RELAY_LAG = 6
 CODE = 5600.0
 NT = (((1,), (1,)), ((), ()))

time: 71.9 us -> 71.4 us (level)
  Pallas kernels: 69.3 us -> 68.4 us
    pallas_call x1, Pallas kernels: 69.3 us -> 68.4 us  [shards(): pl.pallas_call(functools.partial(kernel, frame_count, mod_count), out_sha...]
where the time goes in v8:
time: 71.4 us; the launch traced here: 70.8 us
  Pallas kernels  68.4 us (96%)
  local copies, waits for them, and re-layouts  2.41 us (3%)
    pallas_call x1, Pallas kernels, shards(): pl.pallas_call(functools.partial(kernel, frame_count, mod_count), out_sha...  68.4 us
    unnamed x5, local copies, waits for them, and re-layouts  2.41 us

profile of v8, /device:TPU:1, one launch (start us, length us, event | category | flops | bytes accessed | tf_op | source)
XLA Modules:
  0.0 70.8 jit_solution(5591531501881178016)
XLA Ops:
  0.0 0.0 copy-start
  0.0 0.7 %copy-done = s32[4096]{0:T(1024)S(1)} copy-done((s32[4096]{0:T(1024)S(1)}, s32[4096]{0:T(1024)}, u32[]{:S(2)}) %copy-start) | copy-done | bytes 16408
  0.7 0.0 copy-start.1
  0.7 0.7 %copy-done.1 = s32[4096]{0:T(1024)S(1)} copy-done((s32[4096]{0:T(1024)S(1)}, s32[4096]{0:T(1024)}, u32[]{:S(2)}) %copy-start.1) | copy-done | bytes 16408
  1.4 68.4 %shard_map.37 = f32[2,128,1024]{2,1,0:T(8,128)S(1)} custom-call(bf16[128,4096]{1,0:T(8,128)(2,1)} %frames_hbm.1, s32[32,128]{1,0:T(8,128)S(1)} %bitcast.2, s32[32,128]{1,0:T(8,128)S(1)} %bitcast.3), custom_call_target="tpu_custom_call" | custom-call | tf_op jit(solution)/shard_map/pallas_call | solution.py:561
  69.8 1.0 %copy.5 = f32[2,128,1024]{2,1,0:T(8,128)} copy(f32[2,128,1024]{2,1,0:T(8,128)S(1)} %shard_map.37) | data formatting | bytes 2097152
Async XLA Ops:
  0.0 0.7 %copy-start = (s32[4096]{0:T(1024)S(1)}, s32[4096]{0:T(1024)}, u32[]{:S(2)}) copy-start(s32[4096]{0:T(1024)} %param.4) | copy-start | bytes 49156
  0.7 0.7 %copy-start.1 = (s32[4096]{0:T(1024)S(1)}, s32[4096]{0:T(1024)}, u32[]{:S(2)}) copy-start(s32[4096]{0:T(1024)} %param.5) | copy-start | bytes 49156
